TPU v7x, 32 devices: a whole 2x2x4 slice. The times are simulated.
32 devices in a mesh: dp: 4 (over y, x), seq: 8 (over z, core).
Axes of the slice: x: 2, y: 2, z: 4, core: 2. Of those that a mesh axis runs over, the one named last changes fastest.
Arguments:
- tokens: bfloat16 [4, 16, 16, 4, 512], P('dp', 'seq'), may hold values from -6 to 6
- conv_first: bfloat16 [27, 512, 128], replicated, may hold values from -0.0546875 to 0.0546875
- bias_first: float32 [128], replicated, may hold values from -3 to 3
- conv_second: bfloat16 [27, 128, 384], replicated, may hold values from -0.109375 to 0.109375
- bias_second: float32 [384], replicated, may hold values from -3 to 3
- pixels: bfloat16 [4, 16, 16, 4, 1536], P('dp', None, 'seq'), may hold values from 0 to 1
- mask_index: int32 [4, 57], P('dp'), may hold values from 0 to 63, as said below
Outputs:
- grad_first: float32 [27, 512, 128], P(None, 'seq', 'dp')
- grad_second: float32 [27, 128, 384], P(None, 'seq', 'dp')
Inputs may be any that keep to these rules, and one draw needn't show every extreme that they name: `mask_index`: each row holds 57 distinct positions of the 16 x 4 token grid.
All inputs are finite; a program needn't handle non-finite values.
Results may differ from a plain program's by a relative error of at most 0.003.
Values may be sent and summed in bfloat16 or wider, within the bound.
A program may use at most 128 MiB of HBM per device.

v0:
```python
import jax
import jax.numpy as jnp
import numpy as np
from jax import lax
from jax.experimental import pallas as pl
from jax.experimental.pallas import tpu as pltpu
from jax.sharding import PartitionSpec as P

F32 = jnp.float32
BF16 = jnp.bfloat16
NT = (((1,), (1,)), ((), ()))
GELU_ROOT = 0.7978845608028654
GELU_CUBE = 0.044715


def floor_half(v):
    return v // 2 if v >= 0 else -1


def make_kernel(dims):
    ndp, nseq, frames, tf, rows, cols, width, mid, values = dims
    n = tf * cols * rows
    plane = cols * rows
    dblk = width // nseq
    cblk = mid // ndp
    vblk = values // ndp
    mblk = mid // nseq
    ndev = ndp * nseq
    nz = nseq // 2
    quarter = ndev // 4
    clip_lanes = nseq * n

    def kernel(tok, w1_hbm, b1, w2_hbm, b2, pix, marks, place_of, tperm, perm, colv, lanev,
               lanes_n, o1, o2,
               w1, w2, xbuf, xall, thalo, pxall, tfield, im1, hsend, hhalo, hfield, im2,
               psend, phalo, csend, call_, htsend, htall, qsend, qrecv, rsend, rall, gsend, gall, acc,
               wsem, th_s, th_r, px_s, px_r, x_s, x_r, hh_s, hh_r, ph_s, ph_r,
               c_s, c_r, ht_s, ht_r, q_s, q_r, r_s, r_r, g_s, g_r):
        dp = lax.axis_index("dp")
        seq = lax.axis_index("seq")
        me = dp * nseq + seq
        chip, core = seq // 2, lax.rem(seq, 2)
        nxt = lax.rem(seq + 1, nseq)
        prv = lax.rem(seq + nseq - 1, nseq)

        def remote(src, dst, ss, rs, d, s):
            return pltpu.make_async_remote_copy(
                src_ref=src, dst_ref=dst, send_sem=ss, recv_sem=rs,
                device_id=(d, s), device_id_type=pl.DeviceIdType.MESH)

        cp1 = pltpu.make_async_copy(w1_hbm, w1, wsem.at[0])
        cp2 = pltpu.make_async_copy(w2_hbm, w2, wsem.at[1])
        cp1.start()
        cp2.start()

        barrier = pltpu.get_barrier_semaphore()

        def greet(o, c):
            t = lax.rem(me + o, ndev)
            pl.semaphore_signal(barrier, inc=1, device_id=(t // nseq, lax.rem(t, nseq)),
                                device_id_type=pl.DeviceIdType.MESH)
            return c

        lax.fori_loop(1, ndev, greet, 0)

        def ordered(frame):
            raw = frame.astype(F32).reshape(plane, width).astype(BF16)
            return jnp.dot(tperm[...], raw, preferred_element_type=F32)

        flat = jnp.concatenate([ordered(tok[t]) for t in range(tf)], axis=0)
        xt = flat.T
        for s in range(nseq):
            xbuf[s] = xt[s * dblk:(s + 1) * dblk].astype(BF16)
        pl.semaphore_wait(barrier, ndev - 1)

        def halo(first, last, dst, ss, rs):
            return (remote(last, dst.at[0], ss.at[0], rs.at[0], dp, nxt),
                    remote(first, dst.at[1], ss.at[1], rs.at[1], dp, prv))

        th = halo(tok.at[0], tok.at[tf - 1], thalo, th_s, th_r)
        for c in th:
            c.start()

        def px_copy(o):
            s = lax.rem(seq + o, nseq)
            return remote(pix.at[pl.ds(s * tf, tf)], pxall.at[seq], px_s.at[o], px_r.at[seq],
                          dp, s)

        def px_arrival(o):
            s = lax.rem(seq + nseq - o, nseq)
            return remote(pix.at[pl.ds(s * tf, tf)], pxall.at[s], px_s.at[o], px_r.at[s], dp, s)

        def x_copy(o):
            t = lax.rem(me + o, ndev)
            s = lax.rem(t, nseq)
            return remote(xbuf.at[s], xall.at[me], x_s.at[o], x_r.at[me], t // nseq, s)

        def x_arrival(o):
            t = lax.rem(me + ndev - o, ndev)
            s = lax.rem(t, nseq)
            return remote(xbuf.at[s], xall.at[t], x_s.at[o], x_r.at[t], t // nseq, s)

        def c_pair(o):
            d = lax.rem(dp + o, ndp)
            return (remote(csend.at[d], call_.at[dp], c_s.at[o], c_r.at[dp], d, seq),
                    remote(htsend, htall.at[dp], ht_s.at[o], ht_r.at[dp], d, seq))

        def c_arrival(o):
            d = lax.rem(dp + ndp - o, ndp)
            return (remote(csend.at[d], call_.at[d], c_s.at[o], c_r.at[d], d, seq),
                    remote(htsend, htall.at[d], ht_s.at[o], ht_r.at[d], d, seq))

        def r_copy(o):
            s = lax.rem(chip + o, nz)
            return remote(rsend.at[s], rall.at[chip], r_s.at[o], r_r.at[chip], dp,
                          s * 2 + core)

        def r_arrival(o):
            s = lax.rem(chip + nz - o, nz)
            return remote(rsend.at[s], rall.at[s], r_s.at[o], r_r.at[s], dp, s * 2 + core)

        def g_copy(o):
            t = lax.rem(me + o, ndev)
            d = t // nseq
            return remote(gsend.at[d], gall.at[me], g_s.at[o], g_r.at[me], d, lax.rem(t, nseq))

        def g_arrival(o):
            t = lax.rem(me + ndev - o, ndev)
            d = t // nseq
            return remote(gsend.at[d], gall.at[t], g_s.at[o], g_r.at[t], d, lax.rem(t, nseq))

        def each(count, act, low=1):
            def body(o, c):
                act(o)
                return c
            lax.fori_loop(low, count, body, 0)

        def start_all(count, copy, low=1):
            each(count, lambda o: copy(o).start(), low)

        def finish(count, copy, arrival):
            each(count, lambda o: copy(o).wait_send())
            each(count, lambda o: arrival(o).wait_recv())

        start_all(nz, px_copy)
        start_all(quarter, x_copy)
        xall[me] = xbuf[seq]
        own = pltpu.make_async_copy(pix.at[pl.ds(seq * tf, tf)], pxall.at[seq], wsem.at[2])
        own.start()

        matches = (place_of[...] == marks[...]).astype(F32)
        scale = 2.0 / (4 * values) * jnp.sum(matches, axis=1, keepdims=True)
        h_low, h_high = colv[:, 1:2], colv[:, 2:3]
        w_low, w_high = colv[:, 3:4], colv[:, 4:5]

        def row_shift(v, d):
            m = v.shape[0]
            if d == 0:
                return v
            rolled = pltpu.roll(v, 1 if d < 0 else m - 1, axis=0)
            return rolled * (h_low if d < 0 else h_high)[:m]

        def col_shift(v, d):
            m = v.shape[0]
            if d == 0:
                return v
            rolled = pltpu.roll(v, rows if d < 0 else m - rows, axis=0)
            return rolled * (w_low if d < 0 else w_high)[:m]

        def place(field, frame, v, count):
            for d in (-1, 0, 1):
                field[d + 1, frame:frame + count, 1:cols + 1] = (
                    row_shift(v, d).astype(BF16).reshape(count, cols, rows, v.shape[1]))

        def edges(field):
            zero = jnp.zeros((3, tf + 2, 1, rows, field.shape[4]), BF16)
            field[:, :, 0:1] = zero
            field[:, :, cols + 1:cols + 2] = zero

        first = jnp.where(seq > 0, 1.0, 0.0).astype(F32)
        final = jnp.where(seq < nseq - 1, 1.0, 0.0).astype(F32)

        edges(tfield)
        edges(hfield)
        place(tfield, 1, flat, tf)
        def taps_first(a):
            for bc in range(9):
                k = a * 9 + bc
                im1[:, k * width:(k + 1) * width] = (
                    tfield[bc // 3, a:a + tf, bc % 3:bc % 3 + cols].reshape(n, width))
            span = slice(a * 9 * width, (a + 1) * 9 * width)
            return jnp.dot(im1[:, span], w1[span], preferred_element_type=F32)

        cp1.wait()
        z = taps_first(1) + b1[...]
        for c in th:
            c.wait()
        place(tfield, 0, ordered(thalo[0]) * first, 1)
        place(tfield, tf + 1, ordered(thalo[1]) * final, 1)
        z = z + taps_first(0) + taps_first(2)
        th_ = jnp.tanh(GELU_ROOT * (z + GELU_CUBE * z * z * z))
        slope = 0.5 * (1.0 + th_) + 0.5 * z * (1.0 - th_ * th_) * GELU_ROOT * (
            1.0 + 3.0 * GELU_CUBE * z * z)
        hid = (0.5 * z * (1.0 + th_)).astype(BF16)
        hsend[...] = hid.reshape(tf, cols, rows, mid)
        hh = halo(hsend.at[0], hsend.at[tf - 1], hhalo, hh_s, hh_r)
        for c in hh:
            c.start()
        hid_f = hid.astype(F32)
        place(hfield, 1, hid_f, tf)

        start_all(nseq, px_copy, nz)

        def taps_second(a):
            for ij in range(4):
                i, j = ij // 2, ij % 2
                for bc in range(9):
                    k = a * 9 + bc
                    dh, dw = floor_half(i + bc // 3 - 1), floor_half(j + bc % 3 - 1)
                    im2[ij * n:(ij + 1) * n, k * mid:(k + 1) * mid] = (
                        hfield[dh + 1, a:a + tf, dw + 1:dw + 1 + cols].reshape(n, mid))
            span = slice(a * 9 * mid, (a + 1) * 9 * mid)
            return jnp.dot(im2[:, span], w2[span], preferred_element_type=F32)

        cp2.wait()
        predict = taps_second(1) + b2[...].reshape(1, values)
        for c in hh:
            c.wait()
        start_all(3 * quarter, x_copy, quarter)
        before = hhalo[0].reshape(plane, mid).astype(F32) * first
        after = hhalo[1].reshape(plane, mid).astype(F32) * final
        time_line = jnp.concatenate([before, hid_f, after], axis=0)
        for a in range(3):
            htsend[a * mid:(a + 1) * mid] = (
                time_line[a * plane:a * plane + n].T.astype(BF16))
        each(ndp, lambda o: c_pair(o)[1].start())
        htall[dp] = htsend[...]
        place(hfield, 0, before, 1)
        place(hfield, tf + 1, after, 1)
        predict = predict + taps_second(0) + taps_second(2)

        own.wait()
        finish(nseq, px_copy, px_arrival)
        pix_rows = pxall[...].astype(F32).reshape(n, 4 * values).astype(BF16)
        px = jnp.dot(perm[...], pix_rows, preferred_element_type=F32)
        center = px - jnp.mean(px, axis=-1, keepdims=True)
        spread = jnp.mean(center * center, axis=-1, keepdims=True)
        normed = center * lax.rsqrt(spread + 1e-06)
        cots = []
        for ij in range(4):
            cot = (scale * (predict[ij * n:(ij + 1) * n]
                            - normed[:, ij * values:(ij + 1) * values])).astype(BF16).astype(F32)
            cots.append(cot)
            turned = cot.T
            for d in range(ndp):
                csend[d, ij] = turned[d * vblk:(d + 1) * vblk].astype(BF16)
        each(ndp, lambda o: c_pair(o)[0].start())
        call_[dp] = csend[dp]

        def pair_sums(low, high, shift):
            return (high + shift(low, 1), low + high, shift(high, -1) + low)

        def cell_sums(parts, rshift, cshift):
            by_col = [pair_sums(parts[j], parts[2 + j], rshift) for j in range(2)]
            return [s for b in range(3)
                    for s in pair_sums(by_col[0][b], by_col[1][b], cshift)]

        sums = [s.astype(BF16) for s in cell_sums(cots, row_shift, col_shift)]
        backs = []
        for a in range(3):
            total = jnp.zeros((n, mid), F32)
            for bc in range(9):
                k = a * 9 + bc
                total = total + lax.dot_general(
                    sums[bc], w2[k * mid:(k + 1) * mid], NT, preferred_element_type=F32)
            backs.append(total)
        psend[0] = backs[2][n - plane:]
        psend[1] = backs[0][:plane]
        ph = halo(psend.at[1], psend.at[0], phalo, ph_s, ph_r)
        for c in ph:
            c.start()
        for c in ph:
            c.wait()
        from_prev, from_next = phalo[0] * first, phalo[1] * final
        if tf > 1:
            late = jnp.concatenate([from_prev, backs[2][:n - plane]], axis=0)
            early = jnp.concatenate([backs[0][plane:], from_next], axis=0)
        else:
            late, early = from_prev, from_next
        grad_z = ((backs[1] + late + early) * slope).astype(BF16).astype(F32).T
        for d in range(ndp):
            gsend[d] = grad_z[d * cblk:(d + 1) * cblk].astype(BF16)
        start_all(ndev, g_copy)
        start_all(ndev, x_copy, 3 * quarter)
        gall[me] = gsend[dp]

        each(ndp, lambda o: [c.wait_send() for c in c_pair(o)])
        each(ndp, lambda o: [c.wait_recv() for c in c_arrival(o)])

        def lane_row(v, d):
            rolled = pltpu.roll(v, 1 if d < 0 else n - 1, axis=1)
            return rolled * (lanes_n[0:1] if d < 0 else lanes_n[1:2])

        def lane_col(v, d):
            rolled = pltpu.roll(v, rows if d < 0 else n - rows, axis=1)
            return rolled * (lanes_n[2:3] if d < 0 else lanes_n[3:4])

        acc[...] = jnp.zeros_like(acc)

        def one_clip(q, carry):
            parts = [call_[q, ij].astype(F32) for ij in range(4)]
            stack = jnp.concatenate(cell_sums(parts, lane_row, lane_col), axis=0).astype(BF16)
            acc[...] += lax.dot_general(htall[q], stack, NT, preferred_element_type=F32)
            return carry

        lax.fori_loop(0, ndp, one_clip, 0)

        def part(a, s):
            return acc[pl.ds(pl.multiple_of(a * mid + s * mblk, 8), mblk)]

        for s in range(nz):
            for a in range(3):
                qsend[s, a] = part(a, 2 * s + 1 - core).astype(BF16)
        swap = remote(qsend, qrecv, q_s.at[0], q_r.at[0], dp, 2 * chip + 1 - core)
        swap.start()
        swap.wait()
        for s in range(nz):
            for a in range(3):
                rsend[s, a] = (part(a, 2 * s + core) + qrecv[s, a].astype(F32)).astype(BF16)
        start_all(nz, r_copy)
        rall[chip] = rsend[chip]

        finish(ndev, x_copy, x_arrival)
        finish(ndev, g_copy, g_arrival)
        o1[...] = jnp.zeros_like(o1)

        def one_first(q, carry):
            base = q * nseq
            g = jnp.concatenate([gall[base + s].astype(F32) for s in range(nseq)], axis=1)
            x = jnp.concatenate([xall[base + s] for s in range(nseq)], axis=1)
            pieces = []
            by_row = []
            for b in range(3):
                d = b - 1
                if d == 0:
                    by_row.append(g)
                else:
                    m = pltpu.roll(g, d % clip_lanes, axis=1)
                    by_row.append(m * (lanev[0:1] if d > 0 else lanev[1:2]))
            grid = {}
            for b in range(3):
                for c in range(3):
                    d = c - 1
                    v = by_row[b]
                    if d != 0:
                        v = pltpu.roll(v, (d * rows) % clip_lanes, axis=1)
                        v = v * (lanev[2:3] if d > 0 else lanev[3:4])
                    grid[b, c] = v
            for a in range(3):
                for b in range(3):
                    for c in range(3):
                        d = a - 1
                        v = grid[b, c]
                        if d != 0:
                            v = pltpu.roll(v, (d * plane) % clip_lanes, axis=1)
                            v = v * (lanev[4:5] if d > 0 else lanev[5:6])
                        pieces.append(v)
            stack = jnp.concatenate(pieces, axis=0).astype(BF16)
            o1[...] += lax.dot_general(stack, x, NT, preferred_element_type=F32)
            return carry

        lax.fori_loop(0, ndp, one_first, 0)

        finish(nz, r_copy, r_arrival)
        total = rall[0].astype(F32)
        for s in range(1, nz):
            total = total + rall[s].astype(F32)
        for a in range(3):
            for bc in range(9):
                o2[a * 9 + bc] = total[a, :, bc * vblk:(bc + 1) * vblk]

    return kernel


def per_device(tokens, conv_first, bias_first, conv_second, bias_second, pixels, mask_index):
    ndp, nseq = lax.axis_size("dp"), lax.axis_size("seq")
    tf, rows, cols, width = tokens.shape[1:]
    frames = tf * nseq
    mid, values = conv_second.shape[1], conv_second.shape[2]
    n = tf * rows * cols
    hb = rows // nseq
    dims = (ndp, nseq, frames, tf, rows, cols, width, mid, values)
    plane = rows * cols
    dblk, cblk, vblk, mblk = width // nseq, mid // ndp, values // ndp, mid // nseq
    ndev = ndp * nseq

    idx = np.arange(n, dtype=np.int32)
    t_of, w_of, h_of = idx // plane, idx // rows % cols, idx % rows
    source = (h_of // hb) * (tf * hb * cols) + t_of * (hb * cols) + (h_of % hb) * cols + w_of
    perm = jnp.asarray(source[:, None] == idx[None, :], BF16)
    flat_place = (h_of * cols + w_of)[:plane]
    tperm = jnp.asarray(flat_place[:, None] == idx[None, :plane], BF16)
    place_of = jnp.asarray((h_of * cols + w_of)[:, None])
    colv = jnp.asarray(np.stack([h_of < 0, h_of > 0, h_of < rows - 1,
                                 w_of > 0, w_of < cols - 1], axis=1), F32)
    lanes_n = jnp.asarray(np.stack([h_of > 0, h_of < rows - 1, w_of > 0, w_of < cols - 1]), F32)
    lid = np.arange(frames * plane, dtype=np.int32)
    tl, wl, hl = lid // plane, lid // rows % cols, lid % rows
    lanev = jnp.asarray(np.stack([hl > 0, hl < rows - 1, wl > 0, wl < cols - 1,
                                  tl > 0, tl < frames - 1]), F32)

    vm = pl.BlockSpec(memory_space=pltpu.VMEM)
    hbm = pl.BlockSpec(memory_space=pl.ANY)

    def dma(k):
        return pltpu.SemaphoreType.DMA((k,))

    scratch = [
        pltpu.VMEM((27 * width, mid), BF16),
        pltpu.VMEM((27 * mid, values), BF16),
        pltpu.VMEM((nseq, dblk, n), BF16),
        pltpu.VMEM((ndev, dblk, n), BF16),
        pltpu.VMEM((2, rows, cols, width), BF16),
        pltpu.VMEM((nseq, tf, hb, cols, 4 * values), BF16),
        pltpu.VMEM((3, tf + 2, cols + 2, rows, width), BF16),
        pltpu.VMEM((n, 27 * width), BF16),
        pltpu.VMEM((tf, cols, rows, mid), BF16),
        pltpu.VMEM((2, cols, rows, mid), BF16),
        pltpu.VMEM((3, tf + 2, cols + 2, rows, mid), BF16),
        pltpu.VMEM((4 * n, 27 * mid), BF16),
        pltpu.VMEM((2, plane, mid), F32),
        pltpu.VMEM((2, plane, mid), F32),
        pltpu.VMEM((ndp, 4, vblk, n), BF16),
        pltpu.VMEM((ndp, 4, vblk, n), BF16),
        pltpu.VMEM((3 * mid, n), BF16),
        pltpu.VMEM((ndp, 3 * mid, n), BF16),
        pltpu.VMEM((nseq // 2, 3, mblk, 9 * vblk), BF16),
        pltpu.VMEM((nseq // 2, 3, mblk, 9 * vblk), BF16),
        pltpu.VMEM((nseq // 2, 3, mblk, 9 * vblk), BF16),
        pltpu.VMEM((nseq // 2, 3, mblk, 9 * vblk), BF16),
        pltpu.VMEM((ndp, cblk, n), BF16),
        pltpu.VMEM((ndev, cblk, n), BF16),
        pltpu.VMEM((3 * mid, 9 * vblk), F32),
        dma(3), dma(2), dma(2), dma(nseq), dma(nseq), dma(ndev), dma(ndev),
        dma(2), dma(2), dma(2), dma(2), dma(ndp), dma(ndp), dma(ndp), dma(ndp),
        dma(1), dma(1), dma(nseq // 2), dma(nseq // 2), dma(ndev), dma(ndev),
    ]
    first, second = pl.pallas_call(
        make_kernel(dims),
        out_shape=(jax.ShapeDtypeStruct((27 * cblk, dblk), F32),
                   jax.ShapeDtypeStruct((27, mblk, vblk), F32)),
        in_specs=[vm, hbm, vm, hbm, vm, hbm, vm, vm, vm, vm, vm, vm, vm],
        out_specs=(vm, vm),
        scratch_shapes=scratch,
        compiler_params=pltpu.CompilerParams(
            collective_id=0, has_side_effects=True, vmem_limit_bytes=60 * 1024 * 1024),
        name="step",
    )(tokens[0], conv_first.reshape(27 * width, mid), bias_first.reshape(1, mid),
      conv_second.reshape(27 * mid, values), bias_second,
      pixels[0], mask_index, place_of, tperm, perm, colv, lanev, lanes_n)
    first = first.reshape(27, cblk, dblk).transpose(0, 2, 1)
    return (first, second)


def solution(mesh):
    return jax.shard_map(
        per_device,
        mesh=mesh,
        in_specs=(
            P("dp", "seq", None, None, None),
            P(),
            P(),
            P(),
            P(),
            P("dp", None, "seq", None, None),
            P("dp", None),
        ),
        out_specs=(P(None, "seq", "dp"), P(None, "seq", "dp")),
        check_vma=False,
    )
```

profile of v0, /device:TPU:0, one launch (start us, length us, event | category | flops | bytes accessed | tf_op | source)
XLA Modules:
  0.0 51.6 jit_solution(7912916037784463973)
XLA Ops:
  0.6 47.5 %step.1 = (f32[864,64]{1,0:T(8,128)}, f32[27,16,96]{2,1,0:T(8,128)}) custom-call(bf16[2,16,4,512]{3,2,1,0:T(4,128)(2,1)} %bitcast.12, bf16[13824,128]{1,0:T(8,128)(2,1)} %bitcast.8, f32[1,128]{1,0:T(1,128)} %bitcast.13, bf16[3456,384]{1,0:T(8,128)(2,1)} %bitcast.9, f32[384]{0:T(512)} %b2.1, bf16[16,2,4,1536]{3,2,1,0:T(4,128)(2,1)} %bitcast.11, ...), custom_call_target="tpu_custom_call" | custom-call | tf_op jit(solution)/shard_map/step/pallas_call | solution.py:448
  48.1 1.8 %copy.17 = f32[27,64,32]{1,2,0:T(8,128)} copy(f32[27,64,32]{1,2,0:T(8,128)} %bitcast.10) | data formatting | bytes 442368
  49.9 1.6 %copy.18 = f32[27,16,96]{2,1,0:T(8,128)} copy(f32[27,16,96]{2,1,0:T(8,128)} %get-tuple-element.9) | data formatting | bytes 331776
where the time goes:
time: 51.8 us; the launch traced here: 51.6 us
  Pallas kernels  47.5 us (92%)
  local copies, waits for them, and re-layouts  3.44 us (7%)
  between operations  0.64 us (1%)
    pallas_call x1, Pallas kernels, per_device(): pl.pallas_call(make_kernel(dims), out_shape=(jax.ShapeDtypeStruct((27 * c...  47.5 us
    unnamed x2, local copies, waits for them, and re-layouts  3.44 us

commit v1 on v0

v1 whole, which is shorter than its diff:
```python
import jax
import jax.numpy as jnp
import numpy as np
from jax import lax
from jax.experimental import pallas as pl
from jax.experimental.pallas import tpu as pltpu
from jax.sharding import PartitionSpec as P

F32 = jnp.float32
BF16 = jnp.bfloat16
NT = (((1,), (1,)), ((), ()))
GELU_ROOT = 0.7978845608028654
GELU_CUBE = 0.044715


def floor_half(v):
    return v // 2 if v >= 0 else -1


def make_kernel(dims):
    ndp, nseq, tf, rows, cols, width, mid, values = dims
    n = tf * cols * rows
    plane = cols * rows
    frames = tf * nseq
    hb = rows // nseq
    he = hb + 2
    line = frames * cols
    ext = he * line
    chunk = tf * cols
    dblk = width // nseq
    cblk = mid // ndp
    vblk = values // ndp
    mblk = mid // nseq
    ndev = ndp * nseq
    nz = nseq // 2
    clip_lanes = nseq * n

    def kernel(tok, w1_hbm, b1, w2_hbm, b2, pix_hbm, marks, place_of, tperm, spread_of, gather_of,
               colv, o1, o2,
               w1, w2, w2b, pixv, xbuf, xall, xs, thalo, tfield, im1, slope_of,
               hsend, hraw, vfield, tgt, cell, psend, praw,
               htsend, htall, lhs, csend, call_, stack, qsend, qrecv, rsend, rall, gsend, gall,
               acc1, acc2,
               wsem, th_s, th_r, h_s, h_r, p_s, p_r, xz_s, xz_r, xd_s, xd_r, ht_s, ht_r,
               c_s, c_r, g_s, g_r, q_s, q_r, r_s, r_r):
        dp = lax.axis_index("dp")
        seq = lax.axis_index("seq")
        me = dp * nseq + seq
        chip, core = seq // 2, lax.rem(seq, 2)

        def remote(src, dst, ss, rs, d, s):
            return pltpu.make_async_remote_copy(
                src_ref=src, dst_ref=dst, send_sem=ss, recv_sem=rs,
                device_id=(d, s), device_id_type=pl.DeviceIdType.MESH)

        def drain(ref, sem):
            pltpu.make_async_copy(ref, ref, sem).wait()

        def each(low, count, act):
            def body(o, c):
                act(o)
                return c
            lax.fori_loop(low, count, body, 0)

        cp1 = pltpu.make_async_copy(w1_hbm, w1, wsem.at[0])
        cp2 = pltpu.make_async_copy(w2_hbm, w2, wsem.at[1])
        cpx = pltpu.make_async_copy(pix_hbm, pixv, wsem.at[2])
        cp1.start()
        cpx.start()
        cp2.start()

        barrier = pltpu.get_barrier_semaphore()

        def greet(o):
            t = lax.rem(me + o, ndev)
            pl.semaphore_signal(barrier, inc=1, device_id=(t // nseq, lax.rem(t, nseq)),
                                device_id_type=pl.DeviceIdType.MESH)

        each(1, ndev, greet)

        for k in range(27):
            a, b, c = k // 9, k // 3 % 3, k % 3
            pltpu.make_async_copy(
                w2_hbm.at[pl.ds(k * mid, mid)],
                w2b.at[b, pl.ds(a * mid, mid), pl.ds(c * values, values)], wsem.at[3]).start()

        def ordered(frame):
            raw = frame.astype(F32).reshape(plane, width).astype(BF16)
            return jnp.dot(tperm[...], raw, preferred_element_type=F32)

        flat = jnp.concatenate([ordered(tok[t]) for t in range(tf)], axis=0)
        xt = flat.T
        for s in range(nseq):
            xbuf[s] = xt[s * dblk:(s + 1) * dblk].astype(BF16)
        pl.semaphore_wait(barrier, ndev - 1)

        up = remote(tok.at[tf - 1], thalo.at[0], th_s.at[0], th_r.at[0], dp,
                    jnp.minimum(seq + 1, nseq - 1))
        down = remote(tok.at[0], thalo.at[1], th_s.at[1], th_r.at[1], dp,
                      jnp.maximum(seq - 1, 0))

        @pl.when(seq < nseq - 1)
        def _():
            up.start()

        @pl.when(seq > 0)
        def _():
            down.start()

        @pl.when(seq == 0)
        def _():
            thalo[0] = jnp.zeros((rows, cols, width), BF16)

        @pl.when(seq == nseq - 1)
        def _():
            thalo[1] = jnp.zeros((rows, cols, width), BF16)

        h_low, h_high = colv[:, 0:1], colv[:, 1:2]

        def row_shift(v, d):
            m = v.shape[0]
            if d == 0:
                return v
            rolled = pltpu.roll(v, 1 if d < 0 else m - 1, axis=0)
            return rolled * (h_low if d < 0 else h_high)[:m]

        def place(field, frame, v, count):
            for d in (-1, 0, 1):
                field[d + 1, frame:frame + count, 1:cols + 1] = (
                    row_shift(v, d).astype(BF16).reshape(count, cols, rows, v.shape[1]))

        zero = jnp.zeros((3, tf + 2, 1, rows, width), BF16)
        tfield[:, :, 0:1] = zero
        tfield[:, :, cols + 1:cols + 2] = zero
        place(tfield, 1, flat, tf)

        def taps_first(a):
            for bc in range(9):
                k = a * 9 + bc
                im1[:, k * width:(k + 1) * width] = (
                    tfield[bc // 3, a:a + tf, bc % 3:bc % 3 + cols].reshape(n, width))
            span = slice(a * 9 * width, (a + 1) * 9 * width)
            return jnp.dot(im1[:, span], w1[span], preferred_element_type=F32)

        cp1.wait()
        z = taps_first(1) + b1[...]

        cpx.wait()
        raw = [pixv[:, h].astype(F32).reshape(line, 4 * values) for h in range(hb)]
        px = jnp.concatenate(raw, axis=0)
        center = px - jnp.mean(px, axis=-1, keepdims=True)
        spread = jnp.mean(center * center, axis=-1, keepdims=True)
        normed = center * lax.rsqrt(spread + 1e-06)
        for ij in range(4):
            tgt[ij] = normed[:, ij * values:(ij + 1) * values] - b2[...].reshape(1, values)
        matches = (place_of[...] + seq * (hb * cols) == marks[...]).astype(F32)
        scale = 2.0 / (4 * values) * jnp.sum(matches, axis=1, keepdims=True)

        @pl.when(seq > 0)
        def _():
            up.wait_recv()

        @pl.when(seq < nseq - 1)
        def _():
            down.wait_recv()

        place(tfield, 0, ordered(thalo[0]), 1)
        place(tfield, tf + 1, ordered(thalo[1]), 1)
        z = z + taps_first(0) + taps_first(2)
        th_ = jnp.tanh(GELU_ROOT * (z + GELU_CUBE * z * z * z))
        hid = (0.5 * z * (1.0 + th_)).astype(BF16)
        hsend[...] = jnp.dot(spread_of[...], hid, preferred_element_type=F32).reshape(
            nseq, he, chunk, mid).astype(BF16)

        def h_copy(o):
            s = lax.rem(seq + o, nseq)
            return remote(hsend.at[s], hraw.at[seq], h_s.at[0], h_r.at[0], dp, s)

        each(1, nseq, lambda o: h_copy(o).start())
        hraw[seq] = hsend[seq]
        slope_of[...] = 0.5 * (1.0 + th_) + 0.5 * z * (1.0 - th_ * th_) * GELU_ROOT * (
            1.0 + 3.0 * GELU_CUBE * z * z)

        def band(size):
            li = lax.broadcasted_iota(jnp.int32, (line, size), 0)
            lw = lax.rem(li, cols)
            return ((lw > 0).astype(F32), (lw < cols - 1).astype(F32),
                    (li >= cols).astype(F32), (li < line - cols).astype(F32))

        w_low, w_high, t_low, t_high = band(mid)
        p_low, p_high, _, _ = band(values)
        le = lax.broadcasted_iota(jnp.int32, (1, ext), 1)
        lw = lax.rem(le, cols)
        lt = lax.rem(le, line)
        e_low, e_high = (lw > 0).astype(F32), (lw < cols - 1).astype(F32)
        s_low, s_high = (lt >= cols).astype(F32), (lt < line - cols).astype(F32)

        def shifted(v, by, mask):
            m = v.shape[0]
            rolled = pltpu.roll(v, (-by) % m, axis=0)
            return (rolled.reshape(m // line, line, v.shape[1]) * mask[None]).reshape(v.shape)

        drain(hraw.at[pl.ds(0, nseq - 1)], h_r.at[0])

        def xz_copy(o):
            s = lax.rem(seq + o, nseq)
            return remote(xbuf.at[s], xall.at[dp, seq], xz_s.at[0], xz_r.at[0], dp, s)

        each(1, nseq, lambda o: xz_copy(o).start())
        xall[dp, seq] = xbuf[seq]

        hin = hraw[...].astype(F32)
        hext = jnp.concatenate(
            [hin[:, hh].reshape(line, mid) for hh in range(he)], axis=0)
        for a in range(3):
            late = hext if a == 1 else shifted(
                hext, cols * (a - 1), t_low if a == 0 else t_high)
            for e in range(3):
                v = late if e == 1 else shifted(late, e - 1, w_low if e == 0 else w_high)
                vfield[a * 3 + e] = v.astype(BF16)
        htsend[...] = hext.T.astype(BF16)

        def ht_copy(o):
            d = lax.rem(dp + o, ndp)
            return remote(htsend, htall.at[dp], ht_s.at[0], ht_r.at[0], d, seq)

        each(1, ndp, lambda o: ht_copy(o).start())
        htall[dp] = htsend[...]

        def taps_second(a):
            parts = []
            for ij in range(4):
                i, j = ij // 2, ij % 2
                cells = []
                for bc in range(9):
                    dh, dw = floor_half(i + bc // 3 - 1), floor_half(j + bc % 3 - 1)
                    low = (1 + dh) * line
                    cells.append(vfield[a * 3 + dw + 1, low:low + hb * line])
                parts.append(jnp.concatenate(cells, axis=1))
            return jnp.dot(jnp.concatenate(parts, axis=0), w2[a * 9 * mid:(a + 1) * 9 * mid],
                           preferred_element_type=F32)

        cp2.wait()
        predict = taps_second(0) + taps_second(1) + taps_second(2)
        cots = []
        for ij in range(4):
            cot = (scale * (predict[ij * n:(ij + 1) * n] - tgt[ij])).astype(BF16).astype(F32)
            cots.append(cot)
            turned = cot.T
            for d in range(ndp):
                csend[d, ij] = turned[d * vblk:(d + 1) * vblk].astype(BF16)

        def c_copy(o):
            d = lax.rem(dp + o, ndp)
            return remote(csend.at[d], call_.at[dp], c_s.at[0], c_r.at[dp], d, seq)

        each(1, ndp, lambda o: c_copy(o).start())
        call_[dp] = csend[dp]

        def pair_sums(low, high, after, before):
            return (high + after(low), low + high, before(high) + low)

        def after_row(v):
            return shifted(v, 1, p_high)

        def before_row(v):
            return shifted(v, -1, p_low)

        for u, (low, high) in enumerate((
                (cots[0], cots[1]), (cots[2], cots[3]),
                (cots[0] + cots[2], cots[1] + cots[3]))):
            for c, s in enumerate(pair_sums(low, high, after_row, before_row)):
                cell[u * n:(u + 1) * n, c * values:(c + 1) * values] = s.astype(BF16)

        drain(w2b, wsem.at[3])
        both = cell[0:2 * n]
        first = lax.dot_general(both, w2b[0], NT, preferred_element_type=F32)
        third = lax.dot_general(both, w2b[2], NT, preferred_element_type=F32)
        second = lax.dot_general(cell[2 * n:3 * n], w2b[1], NT, preferred_element_type=F32)
        same = first[n:] + second + third[:n]
        pieces = []
        for hh in range(he):
            total = None
            for v, dh in ((first[:n], -1), (same, 0), (third[n:], 1)):
                h = hh - 1 - dh
                if 0 <= h < hb:
                    part = v[h * line:(h + 1) * line]
                    total = part if total is None else total + part
            back = total[:, mid:2 * mid]
            back = back + shifted(total[:, :mid], cols, t_high)
            back = back + shifted(total[:, 2 * mid:], -cols, t_low)
            pieces.append(back)
        for hh in range(he):
            psend[:, hh] = pieces[hh].reshape(nseq, chunk, mid).astype(BF16)

        def p_copy(o):
            s = lax.rem(seq + o, nseq)
            return remote(psend.at[s], praw.at[seq], p_s.at[0], p_r.at[0], dp, s)

        each(1, nseq, lambda o: p_copy(o).start())
        praw[seq] = psend[seq]

        drain(xall.at[0, pl.ds(0, nseq - 1)], xz_r.at[0])

        def xd_copy(o):
            d = lax.rem(dp + o, ndp)
            return remote(xall.at[dp], xall.at[dp], xd_s.at[0], xd_r.at[0], d, seq)

        each(1, ndp, lambda o: xd_copy(o).start())

        drain(htall.at[pl.ds(0, ndp - 1)], ht_r.at[0])
        for q in range(ndp):
            turned = htall[q].astype(F32)
            for a in range(3):
                v = turned
                if a != 1:
                    v = pltpu.roll(turned, (cols if a == 0 else ext - cols), axis=1)
                    v = v * (s_low if a == 0 else s_high)
                lhs[:, a, :, q * ext:(q + 1) * ext] = v.reshape(nseq, mblk, ext).astype(BF16)

        def lane_after(v):
            return pltpu.roll(v, ext - 1, axis=1) * e_high

        def lane_before(v):
            return pltpu.roll(v, 1, axis=1) * e_low

        pad = jnp.zeros((vblk, ext - hb * line), F32)

        def clip_stack(q):
            by_col = []
            for j in range(2):
                low, high = [jnp.concatenate([call_[q, i * 2 + j].astype(F32), pad], axis=1)
                             for i in range(2)]
                low_in, high_in = pltpu.roll(low, line, axis=1), pltpu.roll(high, line, axis=1)
                high_out = pltpu.roll(high, 2 * line, axis=1)
                by_col.append((low + high_in, low_in + high_in, low_in + high_out))
            at = pl.ds(pl.multiple_of(q * ext, 128), ext)
            k = 0
            for b in range(3):
                for s in pair_sums(by_col[0][b], by_col[1][b], lane_after, lane_before):
                    stack[k * vblk:(k + 1) * vblk, at] = s.astype(BF16)
                    k += 1

        clip_stack(dp)

        drain(praw.at[pl.ds(0, nseq - 1)], p_r.at[0])
        got = praw[...].astype(F32).reshape(nseq * he * chunk, mid).astype(BF16)
        grad_h = jnp.dot(gather_of[...], got, preferred_element_type=F32)
        grad_z = (grad_h * slope_of[...]).astype(BF16).astype(F32).T
        for d in range(ndp):
            gsend[d] = grad_z[d * cblk:(d + 1) * cblk].astype(BF16)

        def g_copy(o):
            t = lax.rem(me + o, ndev)
            d = t // nseq
            return remote(gsend.at[d], gall.at[dp, seq], g_s.at[0], g_r.at[dp], d,
                          lax.rem(t, nseq))

        each(1, ndev, lambda o: g_copy(o).start())
        gall[dp, seq] = gsend[dp]

        def other_clip(o):
            q = lax.rem(dp + o, ndp)
            drain(call_.at[q], c_r.at[q])
            clip_stack(q)

        each(1, ndp, other_clip)

        def half(k):
            block = jnp.concatenate(
                [lhs[2 * s + k].reshape(3 * mblk, ndp * ext) for s in range(nz)], axis=0)
            return lax.dot_general(block, stack[...], NT, preferred_element_type=F32)

        sent = half(1 - core)
        for s in range(nz):
            qsend[s] = sent[s * 3 * mblk:(s + 1) * 3 * mblk].astype(BF16)
        swap = remote(qsend, qrecv, q_s.at[0], q_r.at[0], dp, 2 * chip + 1 - core)
        swap.start()
        acc2[...] = half(core)

        drain(xall.at[pl.ds(0, ndp - 1)], xd_r.at[0])
        lx = lax.broadcasted_iota(jnp.int32, (1, clip_lanes), 1)
        x_low, x_high = (lx >= plane).astype(F32), (lx < clip_lanes - plane).astype(F32)

        def turn_clip(q):
            x = jnp.concatenate([xall[q, s] for s in range(nseq)], axis=1)
            xf = x.astype(F32)
            xs[q, 0:dblk] = (pltpu.roll(xf, plane, axis=1) * x_low).astype(BF16)
            xs[q, dblk:2 * dblk] = x
            xs[q, 2 * dblk:3 * dblk] = (
                pltpu.roll(xf, clip_lanes - plane, axis=1) * x_high).astype(BF16)

        swap.wait_recv()
        for s in range(nz):
            rsend[s] = (acc2[s * 3 * mblk:(s + 1) * 3 * mblk] + qrecv[s].astype(F32)).astype(BF16)

        def r_copy(o):
            s = lax.rem(chip + o, nz)
            return remote(rsend.at[s], rall.at[chip], r_s.at[0], r_r.at[0], dp, s * 2 + core)

        each(1, nz, lambda o: r_copy(o).start())
        rall[chip] = rsend[chip]
        each(0, ndp, turn_clip)

        lh = lax.rem(lx, rows)
        lc = lax.rem(lx, plane)
        g_h = ((lh < rows - 1).astype(F32), None, (lh > 0).astype(F32))
        g_w = ((lc < plane - rows).astype(F32), None, (lc >= rows).astype(F32))
        acc1[...] = jnp.zeros_like(acc1)

        def one_first(q):
            g = jnp.concatenate([gall[q, s].astype(F32) for s in range(nseq)], axis=1)
            grid = []
            for b in range(3):
                v = g if b == 1 else pltpu.roll(g, (b - 1) % clip_lanes, axis=1) * g_h[b]
                for c in range(3):
                    u = v if c == 1 else pltpu.roll(
                        v, ((c - 1) * rows) % clip_lanes, axis=1) * g_w[c]
                    grid.append(u.astype(BF16))
            acc1[...] += lax.dot_general(jnp.concatenate(grid, axis=0), xs[q], NT,
                                         preferred_element_type=F32)

        drain(gall.at[0, pl.ds(0, nseq - 1)], g_r.at[dp])
        one_first(dp)

        def other_first(o):
            q = lax.rem(dp + o, ndp)
            drain(gall.at[q], g_r.at[q])
            one_first(q)

        each(1, ndp, other_first)
        for a in range(3):
            o1[a * 9 * cblk:(a + 1) * 9 * cblk] = acc1[:, a * dblk:(a + 1) * dblk]

        @pl.when(seq < nseq - 1)
        def _():
            up.wait_send()

        @pl.when(seq > 0)
        def _():
            down.wait_send()

        drain(hsend.at[pl.ds(0, nseq - 1)], h_s.at[0])
        drain(xbuf.at[pl.ds(0, nseq - 1)], xz_s.at[0])
        drain(htall.at[pl.ds(0, ndp - 1)], ht_s.at[0])
        drain(csend.at[pl.ds(0, ndp - 1)], c_s.at[0])
        drain(psend.at[pl.ds(0, nseq - 1)], p_s.at[0])
        drain(xall.at[pl.ds(0, ndp - 1)], xd_s.at[0])
        swap.wait_send()
        for o in range(ndp):
            drain(gall.at[0, pl.ds(0, nseq - 1)] if o == 0 else gall.at[0], g_s.at[0])
        drain(rall.at[pl.ds(0, nz - 1)], r_r.at[0])
        total = rall[0].astype(F32)
        for s in range(1, nz):
            total = total + rall[s].astype(F32)
        for a in range(3):
            for bc in range(9):
                o2[a * 9 + bc] = total[a * mblk:(a + 1) * mblk, bc * vblk:(bc + 1) * vblk]
        drain(rsend.at[pl.ds(0, nz - 1)], r_s.at[0])

    return kernel


def flush(a, b, oa, ob, sem):
    moves = (pltpu.make_async_copy(a, oa, sem.at[0]), pltpu.make_async_copy(b, ob, sem.at[1]))
    for m in moves:
        m.start()
    for m in moves:
        m.wait()


def per_device(tokens, conv_first, bias_first, conv_second, bias_second, pixels, mask_index):
    ndp, nseq = lax.axis_size("dp"), lax.axis_size("seq")
    tf, rows, cols, width = tokens.shape[1:]
    frames = tf * nseq
    mid, values = conv_second.shape[1], conv_second.shape[2]
    n = tf * rows * cols
    hb = rows // nseq
    he = hb + 2
    line = frames * cols
    ext = he * line
    chunk = tf * cols
    dims = (ndp, nseq, tf, rows, cols, width, mid, values)
    plane = rows * cols
    dblk, cblk, vblk, mblk = width // nseq, mid // ndp, values // ndp, mid // nseq
    nz = nseq // 2

    idx = np.arange(n, dtype=np.int32)
    t_of, w_of, h_of = idx // plane, idx // rows % cols, idx % rows
    flat_place = (h_of * cols + w_of)[:plane]
    tperm = jnp.asarray(flat_place[:, None] == idx[None, :plane], BF16)
    msg = np.arange(nseq * he * chunk, dtype=np.int32)
    m_s, m_h = msg // (he * chunk), msg // chunk % he
    m_t, m_w = msg % chunk // cols, msg % cols
    m_row = m_s * hb + m_h - 1
    same = ((m_row[:, None] == h_of[None]) & (m_t[:, None] == t_of[None])
            & (m_w[:, None] == w_of[None]))
    spread_of = jnp.asarray(same, BF16)
    gather_of = jnp.asarray(same.T, BF16)
    own = np.arange(hb * line, dtype=np.int32)
    place_of = jnp.asarray((own // line * cols + own % cols)[:, None])
    colv = jnp.asarray(np.stack([h_of > 0, h_of < rows - 1], axis=1), F32)

    vm = pl.BlockSpec(memory_space=pltpu.VMEM)
    hbm = pl.BlockSpec(memory_space=pl.ANY)

    def dma(k):
        return pltpu.SemaphoreType.DMA((k,))

    scratch = [
        pltpu.VMEM((27 * width, mid), BF16),
        pltpu.VMEM((27 * mid, values), BF16),
        pltpu.VMEM((3, 3 * mid, 3 * values), BF16),
        pltpu.VMEM((frames, hb, cols, 4 * values), BF16),
        pltpu.VMEM((nseq, dblk, n), BF16),
        pltpu.VMEM((ndp, nseq, dblk, n), BF16),
        pltpu.VMEM((ndp, 3 * dblk, nseq * n), BF16),
        pltpu.VMEM((2, rows, cols, width), BF16),
        pltpu.VMEM((3, tf + 2, cols + 2, rows, width), BF16),
        pltpu.VMEM((n, 27 * width), BF16),
        pltpu.VMEM((n, mid), F32),
        pltpu.VMEM((nseq, he, chunk, mid), BF16),
        pltpu.VMEM((nseq, he, chunk, mid), BF16),
        pltpu.VMEM((9, ext, mid), BF16),
        pltpu.VMEM((4, n, values), F32),
        pltpu.VMEM((3 * n, 3 * values), BF16),
        pltpu.VMEM((nseq, he, chunk, mid), BF16),
        pltpu.VMEM((nseq, he, chunk, mid), BF16),
        pltpu.VMEM((mid, ext), BF16),
        pltpu.VMEM((ndp, mid, ext), BF16),
        pltpu.VMEM((nseq, 3, mblk, ndp * ext), BF16),
        pltpu.VMEM((ndp, 4, vblk, n), BF16),
        pltpu.VMEM((ndp, 4, vblk, n), BF16),
        pltpu.VMEM((9 * vblk, ndp * ext), BF16),
        pltpu.VMEM((nz, 3 * mblk, 9 * vblk), BF16),
        pltpu.VMEM((nz, 3 * mblk, 9 * vblk), BF16),
        pltpu.VMEM((nz, 3 * mblk, 9 * vblk), BF16),
        pltpu.VMEM((nz, 3 * mblk, 9 * vblk), BF16),
        pltpu.VMEM((ndp, cblk, n), BF16),
        pltpu.VMEM((ndp, nseq, cblk, n), BF16),
        pltpu.VMEM((9 * cblk, 3 * dblk), F32),
        pltpu.VMEM((nz * 3 * mblk, 9 * vblk), F32),
        dma(4), dma(2), dma(2), dma(1), dma(1), dma(1), dma(1), dma(1), dma(1), dma(1), dma(1),
        dma(1), dma(1), dma(1), dma(ndp), dma(1), dma(ndp), dma(1), dma(1), dma(1), dma(1),
    ]
    first, second = pl.pallas_call(
        make_kernel(dims),
        out_shape=(pltpu.VMEM((27 * cblk, dblk), F32), pltpu.VMEM((27, mblk, vblk), F32)),
        in_specs=[vm, hbm, vm, hbm, vm, hbm, vm, vm, vm, vm, vm, vm],
        out_specs=(vm, vm),
        scratch_shapes=scratch,
        compiler_params=pltpu.CompilerParams(
            collective_id=0, has_side_effects=True, vmem_limit_bytes=60 * 1024 * 1024),
        name="step",
    )(tokens[0], conv_first.reshape(27 * width, mid), bias_first.reshape(1, mid),
      conv_second.reshape(27 * mid, values), bias_second,
      pixels[0], mask_index, place_of, tperm, spread_of, gather_of, colv)
    first, second = pl.pallas_call(
        flush,
        out_shape=(jax.ShapeDtypeStruct(first.shape, F32), jax.ShapeDtypeStruct(second.shape, F32)),
        in_specs=[vm, vm],
        out_specs=(hbm, hbm),
        scratch_shapes=[dma(2)],
        compiler_params=pltpu.CompilerParams(vmem_limit_bytes=4 * 1024 * 1024),
        name="flush",
    )(pltpu.with_memory_space_constraint(first, pltpu.VMEM),
      pltpu.with_memory_space_constraint(second, pltpu.VMEM))
    first = first.reshape(27, cblk, dblk).transpose(0, 2, 1)
    return (first, second)


def solution(mesh):
    return jax.shard_map(
        per_device,
        mesh=mesh,
        in_specs=(
            P("dp", "seq", None, None, None),
            P(),
            P(),
            P(),
            P(),
            P("dp", None, "seq", None, None),
            P("dp", None),
        ),
        out_specs=(P(None, "seq", "dp"), P(None, "seq", "dp")),
        check_vma=False,
    )
```

time: 51.8 us -> 42.1 us (0.81)
  Pallas kernels: 47.5 us -> 41.3 us
  local copies, waits for them, and re-layouts: 3.44 us -> 0 us
    pallas_call x1 -> x2, Pallas kernels: 47.5 us -> 41.3 us  [the longest x1 40.5 us: per_device(): pl.pallas_call(make_kernel(dims), out_shape=(pltpu.VMEM((27 * cblk, dblk)...]
    unnamed x2 -> x0, local copies, waits for them, and re-layouts: 3.44 us -> none
where the time goes in v1:
time: 42.1 us; the launch traced here: 42 us
  Pallas kernels  41.3 us (98%)
  between operations  0.64 us (2%)
    pallas_call x1, Pallas kernels, per_device(): pl.pallas_call(make_kernel(dims), out_shape=(pltpu.VMEM((27 * cblk, dblk)...  40.5 us
    pallas_call x1, Pallas kernels, per_device(): pl.pallas_call(flush, out_shape=(jax.ShapeDtypeStruct(first.shape, F32),...  0.85 us

profile of v1, /device:TPU:0, one launch (start us, length us, event | category | flops | bytes accessed | tf_op | source)
XLA Modules:
  0.0 42.0 jit_solution(13560941401776167035)
XLA Ops:
  0.6 40.5 %step.1 = (f32[864,64]{1,0:T(8,128)S(1)}, f32[27,16,96]{2,1,0:T(8,128)S(1)}) custom-call(bf16[2,16,4,512]{3,2,1,0:T(4,128)(2,1)} %bitcast.11, bf16[13824,128]{1,0:T(8,128)(2,1)} %bitcast.8, f32[1,128]{1,0:T(1,128)} %bitcast.12, bf16[3456,384]{1,0:T(8,128)(2,1)} %bitcast.9, f32[384]{0:T(512)} %b2.1, bf16[16,2,4,1536]{3,2,1,0:T(4,128)(2,1)} %bitcast.10, ...), custom_call_target="tpu_custom_call" | custom-call | tf_op jit(solution)/shard_map/step/pallas_call | solution.py:546
  41.1 0.9 %flush.1 = (f32[864,64]{1,0:T(8,128)}, f32[27,16,96]{2,1,0:T(8,128)}) custom-call(f32[864,64]{1,0:T(8,128)S(1)} %get-tuple-element.6.a, f32[27,16,96]{2,1,0:T(8,128)S(1)} %get-tuple-element.7.b), custom_call_target="tpu_custom_call" | custom-call | tf_op jit(solution)/shard_map/flush/pallas_call | solution.py:558

commit v2 on v1

--- a/solution.py
+++ b/solution.py
@@ -35,14 +35,15 @@
     nz = nseq // 2
     clip_lanes = nseq * n
 
-    def kernel(tok, w1_hbm, b1, w2_hbm, b2, pix_hbm, marks, place_of, tperm, spread_of, gather_of,
-               colv, o1, o2,
-               w1, w2, w2b, pixv, xbuf, xall, xs, thalo, tfield, im1, slope_of,
+    def kernel(tok_hbm, w1_hbm, b1_hbm, w2_hbm, b2_hbm, pix_hbm, marks_hbm, tperm_hbm, spread_hbm,
+               gather_hbm, o1, o2,
+               tok, b1, b2, marks, tperm, spread_of, gather_of,
+               w1, w2, w2b, weff, pixv, xbuf, xall, xs, tsend, thalo, tfield, im1, slope_of,
                hsend, hraw, vfield, tgt, cell, psend, praw,
                htsend, htall, lhs, csend, call_, stack, qsend, qrecv, rsend, rall, gsend, gall,
                acc1, acc2,
                wsem, th_s, th_r, h_s, h_r, p_s, p_r, xz_s, xz_r, xd_s, xd_r, ht_s, ht_r,
-               c_s, c_r, g_s, g_r, q_s, q_r, r_s, r_r):
+               c_s, c_r, g_s, g_r, f_s, f_r, q_s, q_r, r_s, r_r):
         dp = lax.axis_index("dp")
         seq = lax.axis_index("seq")
         me = dp * nseq + seq
@@ -62,13 +63,6 @@
                 return c
             lax.fori_loop(low, count, body, 0)
 
-        cp1 = pltpu.make_async_copy(w1_hbm, w1, wsem.at[0])
-        cp2 = pltpu.make_async_copy(w2_hbm, w2, wsem.at[1])
-        cpx = pltpu.make_async_copy(pix_hbm, pixv, wsem.at[2])
-        cp1.start()
-        cpx.start()
-        cp2.start()
-
         barrier = pltpu.get_barrier_semaphore()
 
         def greet(o):
@@ -76,76 +70,78 @@
             pl.semaphore_signal(barrier, inc=1, device_id=(t // nseq, lax.rem(t, nseq)),
                                 device_id_type=pl.DeviceIdType.MESH)
 
+        loads = [pltpu.make_async_copy(src, dst, wsem.at[k]) for k, (src, dst) in enumerate((
+            (tok_hbm, tok), (tperm_hbm, tperm), (b1_hbm, b1), (b2_hbm, b2), (marks_hbm, marks),
+            (spread_hbm, spread_of), (gather_hbm, gather_of), (pix_hbm, pixv), (w2_hbm, w2)))]
+        loads[0].start()
+        loads[1].start()
+        for a in range(3):
+            pltpu.make_async_copy(w1_hbm.at[pl.ds(a * 9 * width, 9 * width)],
+                                  w1.at[:, pl.ds(a * mid, mid)], wsem.at[9]).start()
+        for m in loads[2:]:
+            m.start()
         each(1, ndev, greet)
-
         for k in range(27):
             a, b, c = k // 9, k // 3 % 3, k % 3
             pltpu.make_async_copy(
                 w2_hbm.at[pl.ds(k * mid, mid)],
-                w2b.at[b, pl.ds(a * mid, mid), pl.ds(c * values, values)], wsem.at[3]).start()
+                w2b.at[b, pl.ds(a * mid, mid), pl.ds(c * values, values)], wsem.at[10]).start()
 
         def ordered(frame):
             raw = frame.astype(F32).reshape(plane, width).astype(BF16)
             return jnp.dot(tperm[...], raw, preferred_element_type=F32)
 
+        loads[0].wait()
+        loads[1].wait()
         flat = jnp.concatenate([ordered(tok[t]) for t in range(tf)], axis=0)
         xt = flat.T
         for s in range(nseq):
             xbuf[s] = xt[s * dblk:(s + 1) * dblk].astype(BF16)
-        pl.semaphore_wait(barrier, ndev - 1)
-
-        up = remote(tok.at[tf - 1], thalo.at[0], th_s.at[0], th_r.at[0], dp,
-                    jnp.minimum(seq + 1, nseq - 1))
-        down = remote(tok.at[0], thalo.at[1], th_s.at[1], th_r.at[1], dp,
-                      jnp.maximum(seq - 1, 0))
-
-        @pl.when(seq < nseq - 1)
-        def _():
-            up.start()
-
-        @pl.when(seq > 0)
-        def _():
-            down.start()
-
-        @pl.when(seq == 0)
-        def _():
-            thalo[0] = jnp.zeros((rows, cols, width), BF16)
-
-        @pl.when(seq == nseq - 1)
-        def _():
-            thalo[1] = jnp.zeros((rows, cols, width), BF16)
-
-        h_low, h_high = colv[:, 0:1], colv[:, 1:2]
-
-        def row_shift(v, d):
-            m = v.shape[0]
-            if d == 0:
-                return v
-            rolled = pltpu.roll(v, 1 if d < 0 else m - 1, axis=0)
-            return rolled * (h_low if d < 0 else h_high)[:m]
-
-        def place(field, frame, v, count):
-            for d in (-1, 0, 1):
-                field[d + 1, frame:frame + count, 1:cols + 1] = (
-                    row_shift(v, d).astype(BF16).reshape(count, cols, rows, v.shape[1]))
-
-        zero = jnp.zeros((3, tf + 2, 1, rows, width), BF16)
+
+        lr = lax.broadcasted_iota(jnp.int32, (rows, width), 0)
+        edge = ((lr > 0).astype(F32), None, (lr < rows - 1).astype(F32))
+        zero = jnp.zeros((3, tf, 1, rows, width), BF16)
         tfield[:, :, 0:1] = zero
         tfield[:, :, cols + 1:cols + 2] = zero
-        place(tfield, 1, flat, tf)
-
-        def taps_first(a):
-            for bc in range(9):
-                k = a * 9 + bc
-                im1[:, k * width:(k + 1) * width] = (
-                    tfield[bc // 3, a:a + tf, bc % 3:bc % 3 + cols].reshape(n, width))
-            span = slice(a * 9 * width, (a + 1) * 9 * width)
-            return jnp.dot(im1[:, span], w1[span], preferred_element_type=F32)
-
-        cp1.wait()
-        z = taps_first(1) + b1[...]
-
-        cpx.wait()
+        for b in range(3):
+            v = flat.reshape(tf, cols, rows, width)
+            if b != 1:
+                v = pltpu.roll(flat, 1 if b == 0 else n - 1, axis=0).reshape(
+                    tf * cols, rows, width) * edge[b][None]
+            tfield[b, :, 1:cols + 1] = v.reshape(tf, cols, rows, width).astype(BF16)
+        for bc in range(9):
+            im1[:, bc * width:(bc + 1) * width] = (
+                tfield[bc // 3, :, bc % 3:bc % 3 + cols].reshape(n, width))
+        drain(w1, wsem.at[9])
+        parts = jnp.dot(im1[...], w1[...], preferred_element_type=F32)
+        to_next, here, to_prev = [parts[:, a * mid:(a + 1) * mid] for a in range(3)]
+        tsend[0] = to_next[n - plane:]
+        tsend[1] = to_prev[:plane]
+        pl.semaphore_wait(barrier, ndev - 1)
+
+        up = remote(tsend.at[0], thalo.at[0], th_s.at[0], th_r.at[0], dp,
+                    jnp.minimum(seq + 1, nseq - 1))
+        down = remote(tsend.at[1], thalo.at[1], th_s.at[1], th_r.at[1], dp,
+                      jnp.maximum(seq - 1, 0))
+
+        @pl.when(seq < nseq - 1)
+        def _():
+            up.start()
+
+        @pl.when(seq > 0)
+        def _():
+            down.start()
+
+        @pl.when(seq == 0)
+        def _():
+            thalo[0] = jnp.zeros((plane, mid), F32)
+
+        @pl.when(seq == nseq - 1)
+        def _():
+            thalo[1] = jnp.zeros((plane, mid), F32)
+
+        for m in loads[2:]:
+            m.wait()
         raw = [pixv[:, h].astype(F32).reshape(line, 4 * values) for h in range(hb)]
         px = jnp.concatenate(raw, axis=0)
         center = px - jnp.mean(px, axis=-1, keepdims=True)
@@ -153,9 +149,30 @@
         normed = center * lax.rsqrt(spread + 1e-06)
         for ij in range(4):
             tgt[ij] = normed[:, ij * values:(ij + 1) * values] - b2[...].reshape(1, values)
-        matches = (place_of[...] + seq * (hb * cols) == marks[...]).astype(F32)
+        le = lax.broadcasted_iota(jnp.int32, (n, 1), 0)
+        spot = lax.div(le, line) * cols + lax.rem(le, cols) + seq * (hb * cols)
+        matches = (spot == marks[...]).astype(F32)
         scale = 2.0 / (4 * values) * jnp.sum(matches, axis=1, keepdims=True)
 
+        step = 16 if mid % 16 == 0 else mid
+
+        def sum_taps(o):
+            a, r = lax.div(o, mid // step), lax.rem(o, mid // step)
+            w = [w2[pl.ds(pl.multiple_of((a * 9 + bc) * mid + r * step, step), step)].astype(F32)
+                 for bc in range(9)]
+            wide = []
+            for b in range(3):
+                x, y, z_ = w[b * 3:b * 3 + 3]
+                wide.append((x, y + z_, x + y, z_))
+            for i in range(2):
+                for e in range(4):
+                    x, y, z_ = wide[0][e], wide[1][e], wide[2][e]
+                    for rh, v in enumerate((x, y + z_) if i == 0 else (x + y, z_)):
+                        at = (a * 4 + rh * 2 + e % 2) * mid + r * step
+                        weff[i * 2 + e // 2, pl.ds(pl.multiple_of(at, step), step)] = v.astype(BF16)
+
+        each(0, 3 * (mid // step), sum_taps)
+
         @pl.when(seq > 0)
         def _():
             up.wait_recv()
@@ -164,9 +181,12 @@
         def _():
             down.wait_recv()
 
-        place(tfield, 0, ordered(thalo[0]), 1)
-        place(tfield, tf + 1, ordered(thalo[1]), 1)
-        z = z + taps_first(0) + taps_first(2)
+        if tf > 1:
+            late = jnp.concatenate([thalo[0], to_next[:n - plane]], axis=0)
+            early = jnp.concatenate([to_prev[plane:], thalo[1]], axis=0)
+        else:
+            late, early = thalo[0], thalo[1]
+        z = here + late + early + b1[...]
         th_ = jnp.tanh(GELU_ROOT * (z + GELU_CUBE * z * z * z))
         hid = (0.5 * z * (1.0 + th_)).astype(BF16)
         hsend[...] = jnp.dot(spread_of[...], hid, preferred_element_type=F32).reshape(
@@ -227,24 +247,15 @@
         each(1, ndp, lambda o: ht_copy(o).start())
         htall[dp] = htsend[...]
 
-        def taps_second(a):
-            parts = []
-            for ij in range(4):
-                i, j = ij // 2, ij % 2
-                cells = []
-                for bc in range(9):
-                    dh, dw = floor_half(i + bc // 3 - 1), floor_half(j + bc % 3 - 1)
-                    low = (1 + dh) * line
-                    cells.append(vfield[a * 3 + dw + 1, low:low + hb * line])
-                parts.append(jnp.concatenate(cells, axis=1))
-            return jnp.dot(jnp.concatenate(parts, axis=0), w2[a * 9 * mid:(a + 1) * 9 * mid],
-                           preferred_element_type=F32)
-
-        cp2.wait()
-        predict = taps_second(0) + taps_second(1) + taps_second(2)
         cots = []
         for ij in range(4):
-            cot = (scale * (predict[ij * n:(ij + 1) * n] - tgt[ij])).astype(BF16).astype(F32)
+            i, j = ij // 2, ij % 2
+            near = []
+            for k in range(12):
+                low = (i + k // 2 % 2) * line
+                near.append(vfield[k // 4 * 3 + j + k % 2, low:low + hb * line])
+            predict = jnp.dot(jnp.concatenate(near, axis=1), weff[ij], preferred_element_type=F32)
+            cot = (scale * (predict - tgt[ij])).astype(BF16).astype(F32)
             cots.append(cot)
             turned = cot.T
             for d in range(ndp):
@@ -272,7 +283,7 @@
             for c, s in enumerate(pair_sums(low, high, after_row, before_row)):
                 cell[u * n:(u + 1) * n, c * values:(c + 1) * values] = s.astype(BF16)
 
-        drain(w2b, wsem.at[3])
+        drain(w2b, wsem.at[10])
         both = cell[0:2 * n]
         first = lax.dot_general(both, w2b[0], NT, preferred_element_type=F32)
         third = lax.dot_general(both, w2b[2], NT, preferred_element_type=F32)
@@ -291,7 +302,7 @@
             back = back + shifted(total[:, 2 * mid:], -cols, t_low)
             pieces.append(back)
         for hh in range(he):
-            psend[:, hh] = pieces[hh].reshape(nseq, chunk, mid).astype(BF16)
+            psend[:, hh] = pieces[hh].reshape(nseq, chunk, mid)
 
         def p_copy(o):
             s = lax.rem(seq + o, nseq)
@@ -344,20 +355,23 @@
         clip_stack(dp)
 
         drain(praw.at[pl.ds(0, nseq - 1)], p_r.at[0])
-        got = praw[...].astype(F32).reshape(nseq * he * chunk, mid).astype(BF16)
-        grad_h = jnp.dot(gather_of[...], got, preferred_element_type=F32)
+        got = praw[...].reshape(nseq * he * chunk, mid)
+        major = got.astype(BF16)
+        minor = (got - major.astype(F32)).astype(BF16)
+        grad_h = (jnp.dot(gather_of[...], major, preferred_element_type=F32)
+                  + jnp.dot(gather_of[...], minor, preferred_element_type=F32))
         grad_z = (grad_h * slope_of[...]).astype(BF16).astype(F32).T
         for d in range(ndp):
             gsend[d] = grad_z[d * cblk:(d + 1) * cblk].astype(BF16)
 
         def g_copy(o):
-            t = lax.rem(me + o, ndev)
-            d = t // nseq
-            return remote(gsend.at[d], gall.at[dp, seq], g_s.at[0], g_r.at[dp], d,
-                          lax.rem(t, nseq))
-
-        each(1, ndev, lambda o: g_copy(o).start())
-        gall[dp, seq] = gsend[dp]
+            t = lax.rem(dp * nz + chip + o, ndp * nz)
+            d = t // nz
+            return remote(gsend.at[d], gall.at[dp, core, chip], g_s.at[0], g_r.at[dp], d,
+                          2 * lax.rem(t, nz) + core)
+
+        each(1, ndp * nz, lambda o: g_copy(o).start())
+        gall[dp, core, chip] = gsend[dp]
 
         def other_clip(o):
             q = lax.rem(dp + o, ndp)
@@ -378,7 +392,6 @@
         swap.start()
         acc2[...] = half(core)
 
-        drain(xall.at[pl.ds(0, ndp - 1)], xd_r.at[0])
         lx = lax.broadcasted_iota(jnp.int32, (1, clip_lanes), 1)
         x_low, x_high = (lx >= plane).astype(F32), (lx < clip_lanes - plane).astype(F32)
 
@@ -400,6 +413,20 @@
 
         each(1, nz, lambda o: r_copy(o).start())
         rall[chip] = rsend[chip]
+
+        def g_forward(q):
+            return remote(gall.at[q, core], gall.at[q, core], f_s.at[0], f_r.at[q], dp,
+                          2 * chip + 1 - core)
+
+        def pass_on(o):
+            q = lax.rem(dp + o, ndp)
+            drain(gall.at[0, 0], g_r.at[q])
+            g_forward(q).start()
+
+        drain(gall.at[0, 0, pl.ds(0, nz - 1)], g_r.at[dp])
+        g_forward(dp).start()
+        each(1, ndp, pass_on)
+        drain(xall.at[pl.ds(0, ndp - 1)], xd_r.at[0])
         each(0, ndp, turn_clip)
 
         lh = lax.rem(lx, rows)
@@ -409,7 +436,7 @@
         acc1[...] = jnp.zeros_like(acc1)
 
         def one_first(q):
-            g = jnp.concatenate([gall[q, s].astype(F32) for s in range(nseq)], axis=1)
+            g = jnp.concatenate([gall[q, s % 2, s // 2].astype(F32) for s in range(nseq)], axis=1)
             grid = []
             for b in range(3):
                 v = g if b == 1 else pltpu.roll(g, (b - 1) % clip_lanes, axis=1) * g_h[b]
@@ -420,15 +447,12 @@
             acc1[...] += lax.dot_general(jnp.concatenate(grid, axis=0), xs[q], NT,
                                          preferred_element_type=F32)
 
-        drain(gall.at[0, pl.ds(0, nseq - 1)], g_r.at[dp])
-        one_first(dp)
-
-        def other_first(o):
+        def arrived_first(o):
             q = lax.rem(dp + o, ndp)
-            drain(gall.at[q], g_r.at[q])
+            drain(gall.at[0, 0], f_r.at[q])
             one_first(q)
 
-        each(1, ndp, other_first)
+        each(0, ndp, arrived_first)
         for a in range(3):
             o1[a * 9 * cblk:(a + 1) * 9 * cblk] = acc1[:, a * dblk:(a + 1) * dblk]
 
@@ -448,7 +472,8 @@
         drain(xall.at[pl.ds(0, ndp - 1)], xd_s.at[0])
         swap.wait_send()
         for o in range(ndp):
-            drain(gall.at[0, pl.ds(0, nseq - 1)] if o == 0 else gall.at[0], g_s.at[0])
+            drain(gall.at[0, 0, pl.ds(0, nz - 1)] if o == 0 else gall.at[0, 0], g_s.at[0])
+        drain(gall.at[:, 0], f_s.at[0])
         drain(rall.at[pl.ds(0, nz - 1)], r_r.at[0])
         total = rall[0].astype(F32)
         for s in range(1, nz):
@@ -497,10 +522,6 @@
             & (m_w[:, None] == w_of[None]))
     spread_of = jnp.asarray(same, BF16)
     gather_of = jnp.asarray(same.T, BF16)
-    own = np.arange(hb * line, dtype=np.int32)
-    place_of = jnp.asarray((own // line * cols + own % cols)[:, None])
-    colv = jnp.asarray(np.stack([h_of > 0, h_of < rows - 1], axis=1), F32)
-
     vm = pl.BlockSpec(memory_space=pltpu.VMEM)
     hbm = pl.BlockSpec(memory_space=pl.ANY)
 
@@ -508,24 +529,33 @@
         return pltpu.SemaphoreType.DMA((k,))
 
     scratch = [
-        pltpu.VMEM((27 * width, mid), BF16),
+        pltpu.VMEM((tf, rows, cols, width), BF16),
+        pltpu.VMEM((1, mid), F32),
+        pltpu.VMEM((values,), F32),
+        pltpu.VMEM(mask_index.shape, jnp.int32),
+        pltpu.VMEM((plane, plane), BF16),
+        pltpu.VMEM((nseq * he * chunk, n), BF16),
+        pltpu.VMEM((n, nseq * he * chunk), BF16),
+        pltpu.VMEM((9 * width, 3 * mid), BF16),
         pltpu.VMEM((27 * mid, values), BF16),
         pltpu.VMEM((3, 3 * mid, 3 * values), BF16),
+        pltpu.VMEM((4, 12 * mid, values), BF16),
         pltpu.VMEM((frames, hb, cols, 4 * values), BF16),
         pltpu.VMEM((nseq, dblk, n), BF16),
         pltpu.VMEM((ndp, nseq, dblk, n), BF16),
         pltpu.VMEM((ndp, 3 * dblk, nseq * n), BF16),
-        pltpu.VMEM((2, rows, cols, width), BF16),
-        pltpu.VMEM((3, tf + 2, cols + 2, rows, width), BF16),
-        pltpu.VMEM((n, 27 * width), BF16),
+        pltpu.VMEM((2, plane, mid), F32),
+        pltpu.VMEM((2, plane, mid), F32),
+        pltpu.VMEM((3, tf, cols + 2, rows, width), BF16),
+        pltpu.VMEM((n, 9 * width), BF16),
         pltpu.VMEM((n, mid), F32),
         pltpu.VMEM((nseq, he, chunk, mid), BF16),
         pltpu.VMEM((nseq, he, chunk, mid), BF16),
         pltpu.VMEM((9, ext, mid), BF16),
         pltpu.VMEM((4, n, values), F32),
         pltpu.VMEM((3 * n, 3 * values), BF16),
-        pltpu.VMEM((nseq, he, chunk, mid), BF16),
-        pltpu.VMEM((nseq, he, chunk, mid), BF16),
+        pltpu.VMEM((nseq, he, chunk, mid), F32),
+        pltpu.VMEM((nseq, he, chunk, mid), F32),
         pltpu.VMEM((mid, ext), BF16),
         pltpu.VMEM((ndp, mid, ext), BF16),
         pltpu.VMEM((nseq, 3, mblk, ndp * ext), BF16),
@@ -537,16 +567,17 @@
         pltpu.VMEM((nz, 3 * mblk, 9 * vblk), BF16),
         pltpu.VMEM((nz, 3 * mblk, 9 * vblk), BF16),
         pltpu.VMEM((ndp, cblk, n), BF16),
-        pltpu.VMEM((ndp, nseq, cblk, n), BF16),
+        pltpu.VMEM((ndp, 2, nz, cblk, n), BF16),
         pltpu.VMEM((9 * cblk, 3 * dblk), F32),
         pltpu.VMEM((nz * 3 * mblk, 9 * vblk), F32),
-        dma(4), dma(2), dma(2), dma(1), dma(1), dma(1), dma(1), dma(1), dma(1), dma(1), dma(1),
-        dma(1), dma(1), dma(1), dma(ndp), dma(1), dma(ndp), dma(1), dma(1), dma(1), dma(1),
+        dma(11), dma(2), dma(2), dma(1), dma(1), dma(1), dma(1), dma(1), dma(1), dma(1), dma(1),
+        dma(1), dma(1), dma(1), dma(ndp), dma(1), dma(ndp), dma(1), dma(ndp), dma(1), dma(1),
+        dma(1), dma(1),
     ]
     first, second = pl.pallas_call(
         make_kernel(dims),
         out_shape=(pltpu.VMEM((27 * cblk, dblk), F32), pltpu.VMEM((27, mblk, vblk), F32)),
-        in_specs=[vm, hbm, vm, hbm, vm, hbm, vm, vm, vm, vm, vm, vm],
+        in_specs=[hbm] * 10,
         out_specs=(vm, vm),
         scratch_shapes=scratch,
         compiler_params=pltpu.CompilerParams(
@@ -554,7 +585,7 @@
         name="step",
     )(tokens[0], conv_first.reshape(27 * width, mid), bias_first.reshape(1, mid),
       conv_second.reshape(27 * mid, values), bias_second,
-      pixels[0], mask_index, place_of, tperm, spread_of, gather_of, colv)
+      pixels[0], mask_index, tperm, spread_of, gather_of)
     first, second = pl.pallas_call(
         flush,
         out_shape=(jax.ShapeDtypeStruct(first.shape, F32), jax.ShapeDtypeStruct(second.shape, F32)),

time: 42.1 us -> 36.2 us (0.86); the launches traced: 42 us -> 35.6 us
  Pallas kernels: 41.3 us -> 34.9 us
    pallas_call x1, Pallas kernels: 40.5 us -> 34.1 us  [per_device(): pl.pallas_call(make_kernel(dims), out_shape=(pltpu.VMEM((27 * cblk, dblk)...]
where the time goes in v2:
time: 36.2 us; the launch traced here: 35.6 us
  Pallas kernels  34.9 us (96%)
  between operations  0.64 us (2%)
    pallas_call x1, Pallas kernels, per_device(): pl.pallas_call(make_kernel(dims), out_shape=(pltpu.VMEM((27 * cblk, dblk)...  34.1 us
    pallas_call x1, Pallas kernels, per_device(): pl.pallas_call(flush, out_shape=(jax.ShapeDtypeStruct(first.shape, F32),...  0.85 us

profile of v2, /device:TPU:0, one launch (start us, length us, event | category | flops | bytes accessed | tf_op | source)
XLA Modules:
  0.0 35.6 jit_solution(12405133801868294716)
XLA Ops:
  0.6 34.1 %step.1 = (f32[864,64]{1,0:T(8,128)S(1)}, f32[27,16,96]{2,1,0:T(8,128)S(1)}) custom-call(bf16[2,16,4,512]{3,2,1,0:T(4,128)(2,1)} %bitcast.11, bf16[13824,128]{1,0:T(8,128)(2,1)} %bitcast.8, f32[1,128]{1,0:T(1,128)} %bitcast.12, bf16[3456,384]{1,0:T(8,128)(2,1)} %bitcast.9, f32[384]{0:T(512)} %b2_hbm.1, bf16[16,2,4,1536]{3,2,1,0:T(4,128)(2,1)} %bitcast.10, ...), custom_call_target="tpu_custom_call" | custom-call | tf_op jit(solution)/shard_map/step/pallas_call | solution.py:577
  34.7 0.9 %flush.1 = (f32[864,64]{1,0:T(8,128)}, f32[27,16,96]{2,1,0:T(8,128)}) custom-call(f32[864,64]{1,0:T(8,128)S(1)} %get-tuple-element.6.a, f32[27,16,96]{2,1,0:T(8,128)S(1)} %get-tuple-element.7.b), custom_call_target="tpu_custom_call" | custom-call | tf_op jit(solution)/shard_map/flush/pallas_call | solution.py:589

commit v3 on v2

--- a/solution.py
+++ b/solution.py
@@ -15,6 +15,11 @@
 
 def floor_half(v):
     return v // 2 if v >= 0 else -1
+
+
+def columns(total):
+    half = -(-total // 512) * 256
+    return [(0, half), (half, total - half)] if total > half else [(0, total)]
 
 
 def make_kernel(dims):
@@ -34,20 +39,22 @@
     ndev = ndp * nseq
     nz = nseq // 2
     clip_lanes = nseq * n
+    nk = nz // 2
+    cuts = columns(9 * vblk)
 
     def kernel(tok_hbm, w1_hbm, b1_hbm, w2_hbm, b2_hbm, pix_hbm, marks_hbm, tperm_hbm, spread_hbm,
                gather_hbm, o1, o2,
                tok, b1, b2, marks, tperm, spread_of, gather_of,
                w1, w2, w2b, weff, pixv, xbuf, xall, xs, tsend, thalo, tfield, im1, slope_of,
                hsend, hraw, vfield, tgt, cell, psend, praw,
-               htsend, htall, lhs, csend, call_, stack, qsend, qrecv, rsend, rall, gsend, gall,
-               acc1, acc2,
-               wsem, th_s, th_r, h_s, h_r, p_s, p_r, xz_s, xz_r, xd_s, xd_r, ht_s, ht_r,
-               c_s, c_r, g_s, g_r, f_s, f_r, q_s, q_r, r_s, r_r):
+               hrow, lhs, csend, call_, stack, gsend, gall, acc1, chunks,
+               wsem, th_s, th_r, h_s, h_r, p_s, p_r, xz_s, xz_r, xd_s, xd_r, ht_s, ht_r, e_s, e_r,
+               c_s, c_r, g_s, g_r, f_s, f_r, q_s, q_r, a_s, a_r, b_s, b_r):
         dp = lax.axis_index("dp")
         seq = lax.axis_index("seq")
         me = dp * nseq + seq
         chip, core = seq // 2, lax.rem(seq, 2)
+        qsend, qrecv, asend, arecv, bsend, brecv, acc2 = chunks
 
         def remote(src, dst, ss, rs, d, s):
             return pltpu.make_async_remote_copy(
@@ -63,30 +70,44 @@
                 return c
             lax.fori_loop(low, count, body, 0)
 
+        def peer(o):
+            d, bit = 0, 1
+            while bit < ndp:
+                mine_, other = lax.rem(dp // bit, 2), (o // bit) % 2
+                d = d + bit * (mine_ + other - 2 * mine_ * other)
+                bit = bit * 2
+            return d
+
         barrier = pltpu.get_barrier_semaphore()
 
         def greet(o):
-            t = lax.rem(me + o, ndev)
-            pl.semaphore_signal(barrier, inc=1, device_id=(t // nseq, lax.rem(t, nseq)),
-                                device_id_type=pl.DeviceIdType.MESH)
+            s, d = lax.div(o, ndp), lax.rem(o, ndp)
+
+            @pl.when(jnp.logical_or(s != seq, d != dp))
+            def _():
+                pl.semaphore_signal(barrier, inc=1, device_id=(d, s),
+                                    device_id_type=pl.DeviceIdType.MESH)
 
         loads = [pltpu.make_async_copy(src, dst, wsem.at[k]) for k, (src, dst) in enumerate((
             (tok_hbm, tok), (tperm_hbm, tperm), (b1_hbm, b1), (b2_hbm, b2), (marks_hbm, marks),
             (spread_hbm, spread_of), (gather_hbm, gather_of), (pix_hbm, pixv), (w2_hbm, w2)))]
         loads[0].start()
         loads[1].start()
-        for a in range(3):
-            pltpu.make_async_copy(w1_hbm.at[pl.ds(a * 9 * width, 9 * width)],
-                                  w1.at[:, pl.ds(a * mid, mid)], wsem.at[9]).start()
+        def w1_part(b, a, at):
+            rows_ = 3 * width
+            return pltpu.make_async_copy(
+                w1_hbm.at[pl.ds((a * 9 + b * 3) * width, rows_)],
+                w1.at[pl.ds(b * rows_, rows_), pl.ds(at * mid, mid)],
+                wsem.at[13 if at == 2 else 9 + b])
+
+        for b in range(3):
+            w1_part(b, 0, 0).start()
+            w1_part(b, 2, 1).start()
+        for b in range(3):
+            w1_part(b, 1, 2).start()
+        each(0, ndev, greet)
         for m in loads[2:]:
             m.start()
-        each(1, ndev, greet)
-        for k in range(27):
-            a, b, c = k // 9, k // 3 % 3, k % 3
-            pltpu.make_async_copy(
-                w2_hbm.at[pl.ds(k * mid, mid)],
-                w2b.at[b, pl.ds(a * mid, mid), pl.ds(c * values, values)], wsem.at[10]).start()
-
         def ordered(frame):
             raw = frame.astype(F32).reshape(plane, width).astype(BF16)
             return jnp.dot(tperm[...], raw, preferred_element_type=F32)
@@ -94,10 +115,6 @@
         loads[0].wait()
         loads[1].wait()
         flat = jnp.concatenate([ordered(tok[t]) for t in range(tf)], axis=0)
-        xt = flat.T
-        for s in range(nseq):
-            xbuf[s] = xt[s * dblk:(s + 1) * dblk].astype(BF16)
-
         lr = lax.broadcasted_iota(jnp.int32, (rows, width), 0)
         edge = ((lr > 0).astype(F32), None, (lr < rows - 1).astype(F32))
         zero = jnp.zeros((3, tf, 1, rows, width), BF16)
@@ -112,9 +129,13 @@
         for bc in range(9):
             im1[:, bc * width:(bc + 1) * width] = (
                 tfield[bc // 3, :, bc % 3:bc % 3 + cols].reshape(n, width))
-        drain(w1, wsem.at[9])
-        parts = jnp.dot(im1[...], w1[...], preferred_element_type=F32)
-        to_next, here, to_prev = [parts[:, a * mid:(a + 1) * mid] for a in range(3)]
+        parts = None
+        for b in range(3):
+            span = slice(b * 3 * width, (b + 1) * 3 * width)
+            drain(w1.at[pl.ds(b * 3 * width, 3 * width), pl.ds(0, 2 * mid)], wsem.at[9 + b])
+            part = jnp.dot(im1[:, span], w1[span, 0:2 * mid], preferred_element_type=F32)
+            parts = part if parts is None else parts + part
+        to_next, to_prev = parts[:, :mid], parts[:, mid:]
         tsend[0] = to_next[n - plane:]
         tsend[1] = to_prev[:plane]
         pl.semaphore_wait(barrier, ndev - 1)
@@ -140,7 +161,44 @@
         def _():
             thalo[1] = jnp.zeros((plane, mid), F32)
 
-        for m in loads[2:]:
+        for m in loads[2:7]:
+            m.wait()
+        drain(w1.at[:, pl.ds(2 * mid, mid)], wsem.at[13])
+        slope_of[...] = jnp.dot(im1[...], w1[:, 2 * mid:3 * mid],
+                                preferred_element_type=F32) + b1[...]
+        xt = flat.T
+        for s in range(nseq):
+            xbuf[s] = xt[s * dblk:(s + 1) * dblk].astype(BF16)
+
+        @pl.when(seq > 0)
+        def _():
+            up.wait_recv()
+
+        @pl.when(seq < nseq - 1)
+        def _():
+            down.wait_recv()
+
+        if tf > 1:
+            late = jnp.concatenate([thalo[0], to_next[:n - plane]], axis=0)
+            early = jnp.concatenate([to_prev[plane:], thalo[1]], axis=0)
+        else:
+            late, early = thalo[0], thalo[1]
+        z = slope_of[...] + late + early
+        th_ = jnp.tanh(GELU_ROOT * (z + GELU_CUBE * z * z * z))
+        hid = (0.5 * z * (1.0 + th_)).astype(BF16)
+        hsend[...] = jnp.dot(spread_of[...], hid, preferred_element_type=F32).reshape(
+            nseq, he, chunk, mid).astype(BF16)
+
+        def h_copy(o):
+            s = lax.rem(seq + o, nseq)
+            return remote(hsend.at[s], hraw.at[seq], h_s.at[0], h_r.at[0], dp, s)
+
+        each(1, nseq, lambda o: h_copy(o).start())
+        hraw[seq] = hsend[seq]
+        slope_of[...] = 0.5 * (1.0 + th_) + 0.5 * z * (1.0 - th_ * th_) * GELU_ROOT * (
+            1.0 + 3.0 * GELU_CUBE * z * z)
+
+        for m in loads[7:]:
             m.wait()
         raw = [pixv[:, h].astype(F32).reshape(line, 4 * values) for h in range(hb)]
         px = jnp.concatenate(raw, axis=0)
@@ -158,8 +216,12 @@
 
         def sum_taps(o):
             a, r = lax.div(o, mid // step), lax.rem(o, mid // step)
-            w = [w2[pl.ds(pl.multiple_of((a * 9 + bc) * mid + r * step, step), step)].astype(F32)
-                 for bc in range(9)]
+            w = []
+            for bc in range(9):
+                part = w2[pl.ds(pl.multiple_of((a * 9 + bc) * mid + r * step, step), step)]
+                w2b[bc // 3, pl.ds(pl.multiple_of(a * mid + r * step, step), step),
+                    (bc % 3) * values:(bc % 3 + 1) * values] = part
+                w.append(part.astype(F32))
             wide = []
             for b in range(3):
                 x, y, z_ = w[b * 3:b * 3 + 3]
@@ -173,34 +235,6 @@
 
         each(0, 3 * (mid // step), sum_taps)
 
-        @pl.when(seq > 0)
-        def _():
-            up.wait_recv()
-
-        @pl.when(seq < nseq - 1)
-        def _():
-            down.wait_recv()
-
-        if tf > 1:
-            late = jnp.concatenate([thalo[0], to_next[:n - plane]], axis=0)
-            early = jnp.concatenate([to_prev[plane:], thalo[1]], axis=0)
-        else:
-            late, early = thalo[0], thalo[1]
-        z = here + late + early + b1[...]
-        th_ = jnp.tanh(GELU_ROOT * (z + GELU_CUBE * z * z * z))
-        hid = (0.5 * z * (1.0 + th_)).astype(BF16)
-        hsend[...] = jnp.dot(spread_of[...], hid, preferred_element_type=F32).reshape(
-            nseq, he, chunk, mid).astype(BF16)
-
-        def h_copy(o):
-            s = lax.rem(seq + o, nseq)
-            return remote(hsend.at[s], hraw.at[seq], h_s.at[0], h_r.at[0], dp, s)
-
-        each(1, nseq, lambda o: h_copy(o).start())
-        hraw[seq] = hsend[seq]
-        slope_of[...] = 0.5 * (1.0 + th_) + 0.5 * z * (1.0 - th_ * th_) * GELU_ROOT * (
-            1.0 + 3.0 * GELU_CUBE * z * z)
-
         def band(size):
             li = lax.broadcasted_iota(jnp.int32, (line, size), 0)
             lw = lax.rem(li, cols)
@@ -212,7 +246,6 @@
         le = lax.broadcasted_iota(jnp.int32, (1, ext), 1)
         lw = lax.rem(le, cols)
         lt = lax.rem(le, line)
-        e_low, e_high = (lw > 0).astype(F32), (lw < cols - 1).astype(F32)
         s_low, s_high = (lt >= cols).astype(F32), (lt < line - cols).astype(F32)
 
         def shifted(v, by, mask):
@@ -238,14 +271,16 @@
             for e in range(3):
                 v = late if e == 1 else shifted(late, e - 1, w_low if e == 0 else w_high)
                 vfield[a * 3 + e] = v.astype(BF16)
-        htsend[...] = hext.T.astype(BF16)
+        hrow[dp, 0:hb * line] = hext[line:(hb + 1) * line].astype(BF16)
+        hrow[dp, hb * line:(hb + 1) * line] = hext[0:line].astype(BF16)
+        hrow[dp, (hb + 1) * line:ext] = hext[(hb + 1) * line:ext].astype(BF16)
+        mine = hrow.at[dp, pl.ds(0, hb * line)]
 
         def ht_copy(o):
-            d = lax.rem(dp + o, ndp)
-            return remote(htsend, htall.at[dp], ht_s.at[0], ht_r.at[0], d, seq)
+            d = peer(o)
+            return remote(mine, mine, ht_s.at[0], ht_r.at[0], d, seq)
 
         each(1, ndp, lambda o: ht_copy(o).start())
-        htall[dp] = htsend[...]
 
         cots = []
         for ij in range(4):
@@ -262,7 +297,7 @@
                 csend[d, ij] = turned[d * vblk:(d + 1) * vblk].astype(BF16)
 
         def c_copy(o):
-            d = lax.rem(dp + o, ndp)
+            d = peer(o)
             return remote(csend.at[d], call_.at[dp], c_s.at[0], c_r.at[dp], d, seq)
 
         each(1, ndp, lambda o: c_copy(o).start())
@@ -283,7 +318,6 @@
             for c, s in enumerate(pair_sums(low, high, after_row, before_row)):
                 cell[u * n:(u + 1) * n, c * values:(c + 1) * values] = s.astype(BF16)
 
-        drain(w2b, wsem.at[10])
         both = cell[0:2 * n]
         first = lax.dot_general(both, w2b[0], NT, preferred_element_type=F32)
         third = lax.dot_general(both, w2b[2], NT, preferred_element_type=F32)
@@ -311,49 +345,107 @@
         each(1, nseq, lambda o: p_copy(o).start())
         praw[seq] = psend[seq]
 
-        drain(xall.at[0, pl.ds(0, nseq - 1)], xz_r.at[0])
-
-        def xd_copy(o):
-            d = lax.rem(dp + o, ndp)
-            return remote(xall.at[dp], xall.at[dp], xd_s.at[0], xd_r.at[0], d, seq)
-
-        each(1, ndp, lambda o: xd_copy(o).start())
-
-        drain(htall.at[pl.ds(0, ndp - 1)], ht_r.at[0])
-        for q in range(ndp):
-            turned = htall[q].astype(F32)
-            for a in range(3):
-                v = turned
-                if a != 1:
-                    v = pltpu.roll(turned, (cols if a == 0 else ext - cols), axis=1)
-                    v = v * (s_low if a == 0 else s_high)
-                lhs[:, a, :, q * ext:(q + 1) * ext] = v.reshape(nseq, mblk, ext).astype(BF16)
+        drain(hrow.at[pl.ds(0, ndp - 1), pl.ds(0, hb * line)], ht_r.at[0])
+        others = pl.ds(0, ndp - 1)
+
+        def edge_copy(o, k):
+            q = peer(o)
+            if k == 0:
+                return remote(hrow.at[q, pl.ds((hb - 1) * line, line)],
+                              hrow.at[q, pl.ds(hb * line, line)], e_s.at[0], e_r.at[0], dp,
+                              jnp.minimum(seq + 1, nseq - 1))
+            return remote(hrow.at[q, pl.ds(0, line)],
+                          hrow.at[q, pl.ds((hb + 1) * line, line)], e_s.at[1], e_r.at[1], dp,
+                          jnp.maximum(seq - 1, 0))
+
+        def no_edge(k):
+            def put(o):
+                q = peer(o)
+                hrow[q, (hb + k) * line:(hb + k + 1) * line] = jnp.zeros((line, mid), BF16)
+            each(1, ndp, put)
+
+        @pl.when(seq < nseq - 1)
+        def _():
+            each(1, ndp, lambda o: edge_copy(o, 0).start())
+
+        @pl.when(seq > 0)
+        def _():
+            each(1, ndp, lambda o: edge_copy(o, 1).start())
+
+        @pl.when(seq == 0)
+        def _():
+            no_edge(0)
+
+        @pl.when(seq == nseq - 1)
+        def _():
+            no_edge(1)
+
+        lo = lax.broadcasted_iota(jnp.int32, (1, hb * line), 1)
+        lw = lax.rem(lo, cols)
+        e_low, e_high = (lw > 0).astype(F32), (lw < cols - 1).astype(F32)
+        early_rows, late_rows = (lo < (hb - 1) * line).astype(F32), (lo >= line).astype(F32)
 
         def lane_after(v):
-            return pltpu.roll(v, ext - 1, axis=1) * e_high
+            return pltpu.roll(v, hb * line - 1, axis=1) * e_high
 
         def lane_before(v):
             return pltpu.roll(v, 1, axis=1) * e_low
 
-        pad = jnp.zeros((vblk, ext - hb * line), F32)
+        stack[3 * vblk:6 * vblk] = jnp.zeros((3 * vblk, ndp * ext), BF16)
 
         def clip_stack(q):
-            by_col = []
+            by_col, by_edge = [], []
             for j in range(2):
-                low, high = [jnp.concatenate([call_[q, i * 2 + j].astype(F32), pad], axis=1)
-                             for i in range(2)]
-                low_in, high_in = pltpu.roll(low, line, axis=1), pltpu.roll(high, line, axis=1)
-                high_out = pltpu.roll(high, 2 * line, axis=1)
-                by_col.append((low + high_in, low_in + high_in, low_in + high_out))
-            at = pl.ds(pl.multiple_of(q * ext, 128), ext)
+                low, high = call_[q, j].astype(F32), call_[q, 2 + j].astype(F32)
+                by_col.append((high + pltpu.roll(low, (hb - 1) * line, axis=1) * early_rows,
+                               low + high, low + pltpu.roll(high, line, axis=1) * late_rows))
+                by_edge.append((low * early_rows, None, high * late_rows))
+            base = q * ext
+            at = pl.ds(pl.multiple_of(base, 128), hb * line)
+            rim = pl.ds(pl.multiple_of(base + hb * line, 128), 2 * line)
             k = 0
             for b in range(3):
-                for s in pair_sums(by_col[0][b], by_col[1][b], lane_after, lane_before):
+                inner = pair_sums(by_col[0][b], by_col[1][b], lane_after, lane_before)
+                outer = (None,) * 3 if b == 1 else pair_sums(
+                    by_edge[0][b], by_edge[1][b], lane_after, lane_before)
+                for s, r in zip(inner, outer):
                     stack[k * vblk:(k + 1) * vblk, at] = s.astype(BF16)
+                    if r is not None:
+                        stack[k * vblk:(k + 1) * vblk, rim] = r.astype(BF16)
                     k += 1
 
         clip_stack(dp)
 
+        def clip_lhs(low, high):
+            size = high - low
+            for q in range(ndp):
+                turned = hrow[q, low:high].astype(F32).T
+                for a in range(3):
+                    v = turned
+                    if a != 1:
+                        v = pltpu.roll(turned, (cols if a == 0 else size - cols), axis=1)
+                        v = v * (s_low if a == 0 else s_high)[:, low:high]
+                    lhs[:, a, :, q * ext + low:q * ext + high] = (
+                        v.reshape(nseq, mblk, size).astype(BF16))
+
+        clip_lhs(0, hb * line)
+
+        def other_clip(o):
+            q = peer(o)
+            drain(call_.at[q], c_r.at[q])
+            clip_stack(q)
+
+        each(1, ndp - 1, other_clip)
+
+        @pl.when(seq > 0)
+        def _():
+            drain(hrow.at[others, pl.ds(0, line)], e_r.at[0])
+
+        @pl.when(seq < nseq - 1)
+        def _():
+            drain(hrow.at[others, pl.ds(0, line)], e_r.at[1])
+
+        clip_lhs(hb * line, ext)
         drain(praw.at[pl.ds(0, nseq - 1)], p_r.at[0])
         got = praw[...].reshape(nseq * he * chunk, mid)
         major = got.astype(BF16)
@@ -372,25 +464,60 @@
 
         each(1, ndp * nz, lambda o: g_copy(o).start())
         gall[dp, core, chip] = gsend[dp]
-
-        def other_clip(o):
-            q = lax.rem(dp + o, ndp)
-            drain(call_.at[q], c_r.at[q])
-            clip_stack(q)
-
-        each(1, ndp, other_clip)
-
-        def half(k):
+        drain(xall.at[0, pl.ds(0, nseq - 1)], xz_r.at[0])
+
+        def xd_copy(o):
+            d = peer(o)
+            return remote(xall.at[dp], xall.at[dp], xd_s.at[0], xd_r.at[dp], d, seq)
+
+        each(1, ndp, lambda o: xd_copy(o).start())
+
+        other_clip(ndp - 1)
+
+        def half(k, j):
             block = jnp.concatenate(
                 [lhs[2 * s + k].reshape(3 * mblk, ndp * ext) for s in range(nz)], axis=0)
-            return lax.dot_general(block, stack[...], NT, preferred_element_type=F32)
-
-        sent = half(1 - core)
-        for s in range(nz):
-            qsend[s] = sent[s * 3 * mblk:(s + 1) * 3 * mblk].astype(BF16)
-        swap = remote(qsend, qrecv, q_s.at[0], q_r.at[0], dp, 2 * chip + 1 - core)
-        swap.start()
-        acc2[...] = half(core)
+            low, size = cuts[j]
+            return lax.dot_general(block, stack[low:low + size], NT, preferred_element_type=F32)
+
+        swaps = [remote(qs, qr, q_s.at[j], q_r.at[j], dp, 2 * chip + 1 - core)
+                 for j, (qs, qr) in enumerate(zip(qsend, qrecv))]
+        for j in range(len(cuts)):
+            sent = half(1 - core, j)
+            qsend[j][...] = sent.reshape(nk, 2, 3 * mblk, cuts[j][1]).astype(BF16)
+            swaps[j].start()
+        par, kz = lax.rem(chip, 2), chip // 2
+
+        def near_copy(j, k):
+            return remote(asend[j].at[k], arecv[j].at[k], a_s.at[2 * j], a_r.at[2 * j], dp,
+                          2 * (chip + 1 - 2 * par) + core)
+
+        def last_copy(j):
+            return remote(asend[j].at[kz], arecv[j].at[kz], a_s.at[2 * j + 1], a_r.at[2 * j + 1],
+                          dp, 2 * (chip + 1 - 2 * par) + core)
+
+        def far_copy(j, o):
+            k = lax.rem(kz + o, nk)
+            return remote(bsend[j].at[k], brecv[j].at[kz], b_s.at[j], b_r.at[j], dp,
+                          2 * (2 * k + par) + core)
+
+        for j in range(len(cuts)):
+            size = cuts[j][1]
+            acc2[j][...] = half(core, j).reshape(nk, 2, 3 * mblk, size)
+            swaps[j].wait_recv()
+            asend[j][...] = (acc2[j][:, 1 - par] + qrecv[j][:, 1 - par].astype(F32)).astype(BF16)
+            each(1, nk, lambda o: near_copy(j, lax.rem(kz + o, nk)).start())
+            last_copy(j).start()
+            acc2[j][:, par] = acc2[j][:, par] + qrecv[j][:, par].astype(F32)
+        for j in range(len(cuts)):
+            drain(asend[j].at[pl.ds(0, nk - 1)], a_r.at[2 * j])
+
+            def combine(o):
+                k = lax.rem(kz + o, nk)
+                bsend[j][k] = (acc2[j][k, par] + arecv[j][k].astype(F32)).astype(BF16)
+                far_copy(j, o).start()
+
+            each(1, nk, combine)
 
         lx = lax.broadcasted_iota(jnp.int32, (1, clip_lanes), 1)
         x_low, x_high = (lx >= plane).astype(F32), (lx < clip_lanes - plane).astype(F32)
@@ -403,31 +530,19 @@
             xs[q, 2 * dblk:3 * dblk] = (
                 pltpu.roll(xf, clip_lanes - plane, axis=1) * x_high).astype(BF16)
 
-        swap.wait_recv()
-        for s in range(nz):
-            rsend[s] = (acc2[s * 3 * mblk:(s + 1) * 3 * mblk] + qrecv[s].astype(F32)).astype(BF16)
-
-        def r_copy(o):
-            s = lax.rem(chip + o, nz)
-            return remote(rsend.at[s], rall.at[chip], r_s.at[0], r_r.at[0], dp, s * 2 + core)
-
-        each(1, nz, lambda o: r_copy(o).start())
-        rall[chip] = rsend[chip]
 
         def g_forward(q):
             return remote(gall.at[q, core], gall.at[q, core], f_s.at[0], f_r.at[q], dp,
                           2 * chip + 1 - core)
 
         def pass_on(o):
-            q = lax.rem(dp + o, ndp)
+            q = peer(o)
             drain(gall.at[0, 0], g_r.at[q])
             g_forward(q).start()
 
         drain(gall.at[0, 0, pl.ds(0, nz - 1)], g_r.at[dp])
         g_forward(dp).start()
         each(1, ndp, pass_on)
-        drain(xall.at[pl.ds(0, ndp - 1)], xd_r.at[0])
-        each(0, ndp, turn_clip)
 
         lh = lax.rem(lx, rows)
         lc = lax.rem(lx, plane)
@@ -447,12 +562,18 @@
             acc1[...] += lax.dot_general(jnp.concatenate(grid, axis=0), xs[q], NT,
                                          preferred_element_type=F32)
 
+        turn_clip(dp)
+        drain(gall.at[0, 0], f_r.at[dp])
+        one_first(dp)
+
         def arrived_first(o):
-            q = lax.rem(dp + o, ndp)
+            q = peer(o)
+            drain(xall.at[0], xd_r.at[q])
+            turn_clip(q)
             drain(gall.at[0, 0], f_r.at[q])
             one_first(q)
 
-        each(0, ndp, arrived_first)
+        each(1, ndp, arrived_first)
         for a in range(3):
             o1[a * 9 * cblk:(a + 1) * 9 * cblk] = acc1[:, a * dblk:(a + 1) * dblk]
 
@@ -466,22 +587,43 @@
 
         drain(hsend.at[pl.ds(0, nseq - 1)], h_s.at[0])
         drain(xbuf.at[pl.ds(0, nseq - 1)], xz_s.at[0])
-        drain(htall.at[pl.ds(0, ndp - 1)], ht_s.at[0])
+        drain(hrow.at[pl.ds(0, ndp - 1), pl.ds(0, hb * line)], ht_s.at[0])
         drain(csend.at[pl.ds(0, ndp - 1)], c_s.at[0])
         drain(psend.at[pl.ds(0, nseq - 1)], p_s.at[0])
         drain(xall.at[pl.ds(0, ndp - 1)], xd_s.at[0])
-        swap.wait_send()
+        for w in swaps:
+            w.wait_send()
         for o in range(ndp):
             drain(gall.at[0, 0, pl.ds(0, nz - 1)] if o == 0 else gall.at[0, 0], g_s.at[0])
         drain(gall.at[:, 0], f_s.at[0])
-        drain(rall.at[pl.ds(0, nz - 1)], r_r.at[0])
-        total = rall[0].astype(F32)
-        for s in range(1, nz):
-            total = total + rall[s].astype(F32)
+        @pl.when(seq < nseq - 1)
+        def _():
+            drain(hrow.at[others, pl.ds(0, line)], e_s.at[0])
+
+        @pl.when(seq > 0)
+        def _():
+            drain(hrow.at[others, pl.ds(0, line)], e_s.at[1])
+
+        totals = []
+        for j in range(len(cuts)):
+            drain(asend[j].at[0], a_r.at[2 * j + 1])
+            acc2[j][kz, par] = acc2[j][kz, par] + arecv[j][kz].astype(F32)
+            drain(brecv[j].at[pl.ds(0, nk - 1)], b_r.at[j])
+
+            def add(o):
+                acc2[j][kz, par] = (acc2[j][kz, par]
+                                    + brecv[j][lax.rem(kz + o, nk)].astype(F32))
+
+            each(1, nk, add)
+            totals.append(acc2[j][kz, par])
+        total = jnp.concatenate(totals, axis=1)
         for a in range(3):
             for bc in range(9):
                 o2[a * 9 + bc] = total[a * mblk:(a + 1) * mblk, bc * vblk:(bc + 1) * vblk]
-        drain(rsend.at[pl.ds(0, nz - 1)], r_s.at[0])
+        for j in range(len(cuts)):
+            drain(asend[j].at[pl.ds(0, nk - 1)], a_s.at[2 * j])
+            drain(asend[j].at[0], a_s.at[2 * j + 1])
+            drain(brecv[j].at[pl.ds(0, nk - 1)], b_s.at[j])
 
     return kernel
 
@@ -509,6 +651,7 @@
     plane = rows * cols
     dblk, cblk, vblk, mblk = width // nseq, mid // ndp, values // ndp, mid // nseq
     nz = nseq // 2
+    cuts = columns(9 * vblk)
 
     idx = np.arange(n, dtype=np.int32)
     t_of, w_of, h_of = idx // plane, idx // rows % cols, idx % rows
@@ -556,23 +699,21 @@
         pltpu.VMEM((3 * n, 3 * values), BF16),
         pltpu.VMEM((nseq, he, chunk, mid), F32),
         pltpu.VMEM((nseq, he, chunk, mid), F32),
-        pltpu.VMEM((mid, ext), BF16),
-        pltpu.VMEM((ndp, mid, ext), BF16),
+        pltpu.VMEM((ndp, ext, mid), BF16),
         pltpu.VMEM((nseq, 3, mblk, ndp * ext), BF16),
         pltpu.VMEM((ndp, 4, vblk, n), BF16),
         pltpu.VMEM((ndp, 4, vblk, n), BF16),
         pltpu.VMEM((9 * vblk, ndp * ext), BF16),
-        pltpu.VMEM((nz, 3 * mblk, 9 * vblk), BF16),
-        pltpu.VMEM((nz, 3 * mblk, 9 * vblk), BF16),
-        pltpu.VMEM((nz, 3 * mblk, 9 * vblk), BF16),
-        pltpu.VMEM((nz, 3 * mblk, 9 * vblk), BF16),
         pltpu.VMEM((ndp, cblk, n), BF16),
         pltpu.VMEM((ndp, 2, nz, cblk, n), BF16),
         pltpu.VMEM((9 * cblk, 3 * dblk), F32),
-        pltpu.VMEM((nz * 3 * mblk, 9 * vblk), F32),
-        dma(11), dma(2), dma(2), dma(1), dma(1), dma(1), dma(1), dma(1), dma(1), dma(1), dma(1),
-        dma(1), dma(1), dma(1), dma(ndp), dma(1), dma(ndp), dma(1), dma(ndp), dma(1), dma(1),
-        dma(1), dma(1),
+        [[pltpu.VMEM((nz // 2, 2, 3 * mblk, size), BF16) for _, size in cuts] for _ in range(2)]
+        + [[pltpu.VMEM((nz // 2, 3 * mblk, size), BF16) for _, size in cuts] for _ in range(4)]
+        + [[pltpu.VMEM((nz // 2, 2, 3 * mblk, size), F32) for _, size in cuts]],
+        dma(14), dma(2), dma(2), dma(1), dma(1), dma(1), dma(1), dma(1), dma(1), dma(1), dma(ndp),
+        dma(1), dma(1), dma(2), dma(2), dma(1), dma(ndp), dma(1), dma(ndp), dma(1), dma(ndp),
+        dma(len(cuts)), dma(len(cuts)), dma(2 * len(cuts)), dma(2 * len(cuts)),
+        dma(len(cuts)), dma(len(cuts)),
     ]
     first, second = pl.pallas_call(
         make_kernel(dims),

time: 36.2 us -> 34.9 us (0.964)
  Pallas kernels: 34.9 us -> 33.6 us
    pallas_call x1, Pallas kernels: 34.1 us -> 32.8 us  [per_device(): pl.pallas_call(make_kernel(dims), out_shape=(pltpu.VMEM((27 * cblk, dblk)...]
where the time goes in v3:
time: 34.9 us; the launch traced here: 34.3 us
  Pallas kernels  33.6 us (96%)
  between operations  0.64 us (2%)
    pallas_call x1, Pallas kernels, per_device(): pl.pallas_call(make_kernel(dims), out_shape=(pltpu.VMEM((27 * cblk, dblk)...  32.8 us
    pallas_call x1, Pallas kernels, per_device(): pl.pallas_call(flush, out_shape=(jax.ShapeDtypeStruct(first.shape, F32),...  0.85 us

profile of v3, /device:TPU:0, one launch (start us, length us, event | category | flops | bytes accessed | tf_op | source)
XLA Modules:
  0.0 34.3 jit_solution(14338592196569158367)
XLA Ops:
  0.6 32.8 %step.1 = (f32[864,64]{1,0:T(8,128)S(1)}, f32[27,16,96]{2,1,0:T(8,128)S(1)}) custom-call(bf16[2,16,4,512]{3,2,1,0:T(4,128)(2,1)} %bitcast.11, bf16[13824,128]{1,0:T(8,128)(2,1)} %bitcast.8, f32[1,128]{1,0:T(1,128)} %bitcast.12, bf16[3456,384]{1,0:T(8,128)(2,1)} %bitcast.9, f32[384]{0:T(512)} %b2_hbm.1, bf16[16,2,4,1536]{3,2,1,0:T(4,128)(2,1)} %bitcast.10, ...), custom_call_target="tpu_custom_call" | custom-call | tf_op jit(solution)/shard_map/step/pallas_call | solution.py:718
  33.4 0.9 %flush.1 = (f32[864,64]{1,0:T(8,128)}, f32[27,16,96]{2,1,0:T(8,128)}) custom-call(f32[864,64]{1,0:T(8,128)S(1)} %get-tuple-element.6.a, f32[27,16,96]{2,1,0:T(8,128)S(1)} %get-tuple-element.7.b), custom_call_target="tpu_custom_call" | custom-call | tf_op jit(solution)/shard_map/flush/pallas_call | solution.py:730

commit v4 on v3

--- a/solution.py
+++ b/solution.py
@@ -47,14 +47,15 @@
                tok, b1, b2, marks, tperm, spread_of, gather_of,
                w1, w2, w2b, weff, pixv, xbuf, xall, xs, tsend, thalo, tfield, im1, slope_of,
                hsend, hraw, vfield, tgt, cell, psend, praw,
-               hrow, lhs, csend, call_, stack, gsend, gall, acc1, chunks,
+               hrow, lhs, csend, call_, stack, gsend, gall, acc1, rsend, rall, asend, arecv, bsend, brecv,
+               chunks,
                wsem, th_s, th_r, h_s, h_r, p_s, p_r, xz_s, xz_r, xd_s, xd_r, ht_s, ht_r, e_s, e_r,
-               c_s, c_r, g_s, g_r, f_s, f_r, q_s, q_r, a_s, a_r, b_s, b_r):
+               c_s, c_r, g_s, g_r, f_s, f_r, q_s, q_r, r_s, r_r, a_s, a_r, b_s, b_r):
         dp = lax.axis_index("dp")
         seq = lax.axis_index("seq")
         me = dp * nseq + seq
         chip, core = seq // 2, lax.rem(seq, 2)
-        qsend, qrecv, asend, arecv, bsend, brecv, acc2 = chunks
+        qsend, qrecv, acc2, acc3 = chunks
 
         def remote(src, dst, ss, rs, d, s):
             return pltpu.make_async_remote_copy(
@@ -70,13 +71,16 @@
                 return c
             lax.fori_loop(low, count, body, 0)
 
-        def peer(o):
+        def differ(at, o, size):
             d, bit = 0, 1
-            while bit < ndp:
-                mine_, other = lax.rem(dp // bit, 2), (o // bit) % 2
+            while bit < size:
+                mine_, other = lax.rem(at // bit, 2), (o // bit) % 2
                 d = d + bit * (mine_ + other - 2 * mine_ * other)
                 bit = bit * 2
             return d
+
+        def peer(o):
+            return differ(dp, o, ndp)
 
         barrier = pltpu.get_barrier_semaphore()
 
@@ -393,16 +397,16 @@
 
         stack[3 * vblk:6 * vblk] = jnp.zeros((3 * vblk, ndp * ext), BF16)
 
-        def clip_stack(q):
+        tile = hb * line
+
+        def clip_stack(q, inner_at, outer_at):
             by_col, by_edge = [], []
             for j in range(2):
                 low, high = call_[q, j].astype(F32), call_[q, 2 + j].astype(F32)
                 by_col.append((high + pltpu.roll(low, (hb - 1) * line, axis=1) * early_rows,
                                low + high, low + pltpu.roll(high, line, axis=1) * late_rows))
                 by_edge.append((low * early_rows, None, high * late_rows))
-            base = q * ext
-            at = pl.ds(pl.multiple_of(base, 128), hb * line)
-            rim = pl.ds(pl.multiple_of(base + hb * line, 128), 2 * line)
+            at, rim = pl.ds(inner_at, tile), pl.ds(outer_at, 2 * line)
             k = 0
             for b in range(3):
                 inner = pair_sums(by_col[0][b], by_col[1][b], lane_after, lane_before)
@@ -414,38 +418,42 @@
                         stack[k * vblk:(k + 1) * vblk, rim] = r.astype(BF16)
                     k += 1
 
-        clip_stack(dp)
-
-        def clip_lhs(low, high):
+        clip_stack(dp, 0, (ndp - 1) * tile)
+
+        def clip_lhs(o, low, high, at):
             size = high - low
-            for q in range(ndp):
-                turned = hrow[q, low:high].astype(F32).T
-                for a in range(3):
-                    v = turned
-                    if a != 1:
-                        v = pltpu.roll(turned, (cols if a == 0 else size - cols), axis=1)
-                        v = v * (s_low if a == 0 else s_high)[:, low:high]
-                    lhs[:, a, :, q * ext + low:q * ext + high] = (
-                        v.reshape(nseq, mblk, size).astype(BF16))
-
-        clip_lhs(0, hb * line)
-
-        def other_clip(o):
+            turned = hrow[peer(o), low:high].astype(F32).T
+            for a in range(3):
+                v = turned
+                if a != 1:
+                    v = pltpu.roll(turned, (cols if a == 0 else size - cols), axis=1)
+                    v = v * (s_low if a == 0 else s_high)[:, low:high]
+                lhs[:, a, :, at:at + size] = v.reshape(nseq, mblk, size).astype(BF16)
+
+        for o in range(ndp):
+            clip_lhs(o, 0, tile, (ndp if o == ndp - 1 else o) * tile)
+        clip_lhs(0, tile, ext, (ndp - 1) * tile)
+
+        def other_clip(o, inner_at):
             q = peer(o)
             drain(call_.at[q], c_r.at[q])
-            clip_stack(q)
-
-        each(1, ndp - 1, other_clip)
-
-        @pl.when(seq > 0)
-        def _():
-            drain(hrow.at[others, pl.ds(0, line)], e_r.at[0])
-
-        @pl.when(seq < nseq - 1)
-        def _():
-            drain(hrow.at[others, pl.ds(0, line)], e_r.at[1])
-
-        clip_lhs(hb * line, ext)
+            clip_stack(q, inner_at, pl.multiple_of((ndp + o) * tile, 128))
+
+        each(1, ndp - 1, lambda o: other_clip(o, pl.multiple_of(o * tile, 128)))
+
+        def half(k, j, part):
+            span = slice(part * ndp * tile, (part + 1) * ndp * tile)
+            block = jnp.concatenate(
+                [lhs[2 * s + k, :, :, span].reshape(3 * mblk, ndp * tile) for s in range(nz)],
+                axis=0)
+            low, size = cuts[j]
+            return lax.dot_general(block, stack[low:low + size, span], NT,
+                                   preferred_element_type=F32).reshape(nk, 2, 3 * mblk, size)
+
+        for j in range(len(cuts)):
+            acc3[j][...] = half(1 - core, j, 0)
+            acc2[j][...] = half(core, j, 0)
+
         drain(praw.at[pl.ds(0, nseq - 1)], p_r.at[0])
         got = praw[...].reshape(nseq * he * chunk, mid)
         major = got.astype(BF16)
@@ -472,52 +480,78 @@
 
         each(1, ndp, lambda o: xd_copy(o).start())
 
-        other_clip(ndp - 1)
-
-        def half(k, j):
-            block = jnp.concatenate(
-                [lhs[2 * s + k].reshape(3 * mblk, ndp * ext) for s in range(nz)], axis=0)
-            low, size = cuts[j]
-            return lax.dot_general(block, stack[low:low + size], NT, preferred_element_type=F32)
+        @pl.when(seq > 0)
+        def _():
+            drain(hrow.at[others, pl.ds(0, line)], e_r.at[0])
+
+        @pl.when(seq < nseq - 1)
+        def _():
+            drain(hrow.at[others, pl.ds(0, line)], e_r.at[1])
+
+        for o in range(1, ndp):
+            clip_lhs(o, tile, ext, (ndp + o) * tile)
+        other_clip(ndp - 1, ndp * tile)
 
         swaps = [remote(qs, qr, q_s.at[j], q_r.at[j], dp, 2 * chip + 1 - core)
                  for j, (qs, qr) in enumerate(zip(qsend, qrecv))]
         for j in range(len(cuts)):
-            sent = half(1 - core, j)
-            qsend[j][...] = sent.reshape(nk, 2, 3 * mblk, cuts[j][1]).astype(BF16)
+            qsend[j][...] = (acc3[j][...] + half(1 - core, j, 1)).astype(BF16)
             swaps[j].start()
         par, kz = lax.rem(chip, 2), chip // 2
 
-        def near_copy(j, k):
-            return remote(asend[j].at[k], arecv[j].at[k], a_s.at[2 * j], a_r.at[2 * j], dp,
+        def g_forward(q):
+            return remote(gall.at[q, core], gall.at[q, core], f_s.at[0], f_r.at[q], dp,
+                          2 * chip + 1 - core)
+
+        def pass_on(o):
+            q = peer(o)
+            drain(gall.at[0, 0], g_r.at[q])
+            g_forward(q).start()
+
+        def forward_all():
+            drain(gall.at[0, 0, pl.ds(0, nz - 1)], g_r.at[dp])
+            g_forward(dp).start()
+            each(1, ndp, pass_on)
+
+        def near_copy(k):
+            return remote(asend.at[k], arecv.at[k], a_s.at[0], a_r.at[0], dp,
                           2 * (chip + 1 - 2 * par) + core)
 
-        def last_copy(j):
-            return remote(asend[j].at[kz], arecv[j].at[kz], a_s.at[2 * j + 1], a_r.at[2 * j + 1],
+        def last_copy():
+            return remote(asend.at[kz], arecv.at[kz], a_s.at[1], a_r.at[1],
                           dp, 2 * (chip + 1 - 2 * par) + core)
 
-        def far_copy(j, o):
+        def far_copy(o):
             k = lax.rem(kz + o, nk)
-            return remote(bsend[j].at[k], brecv[j].at[kz], b_s.at[j], b_r.at[j], dp,
+            return remote(bsend.at[k], brecv.at[kz], b_s.at[0], b_r.at[0], dp,
                           2 * (2 * k + par) + core)
 
+        def r_copy(o):
+            t = differ(chip, nz - o, nz)
+            return remote(rsend.at[t // 2, lax.rem(t, 2)], rall.at[chip], r_s.at[0], r_r.at[0],
+                          dp, 2 * t + core)
+
         for j in range(len(cuts)):
-            size = cuts[j][1]
-            acc2[j][...] = half(core, j).reshape(nk, 2, 3 * mblk, size)
+            acc2[j][...] = acc2[j][...] + half(core, j, 1)
             swaps[j].wait_recv()
-            asend[j][...] = (acc2[j][:, 1 - par] + qrecv[j][:, 1 - par].astype(F32)).astype(BF16)
-            each(1, nk, lambda o: near_copy(j, lax.rem(kz + o, nk)).start())
-            last_copy(j).start()
+            if j > 0:
+                rsend[...] = (acc2[j][...] + qrecv[j][...].astype(F32)).astype(BF16)
+                each(1, nz, lambda o: r_copy(o).start())
+                acc2[j][kz, par] = acc2[j][kz, par] + qrecv[j][kz, par].astype(F32)
+                continue
+            asend[...] = (acc2[j][:, 1 - par] + qrecv[j][:, 1 - par].astype(F32)).astype(BF16)
+            each(1, nk, lambda o: near_copy(lax.rem(kz + o, nk)).start())
+            last_copy().start()
             acc2[j][:, par] = acc2[j][:, par] + qrecv[j][:, par].astype(F32)
-        for j in range(len(cuts)):
-            drain(asend[j].at[pl.ds(0, nk - 1)], a_r.at[2 * j])
-
-            def combine(o):
-                k = lax.rem(kz + o, nk)
-                bsend[j][k] = (acc2[j][k, par] + arecv[j][k].astype(F32)).astype(BF16)
-                far_copy(j, o).start()
-
-            each(1, nk, combine)
+        drain(asend.at[pl.ds(0, nk - 1)], a_r.at[0])
+
+        def combine(o):
+            k = lax.rem(kz + o, nk)
+            bsend[k] = (acc2[0][k, par] + arecv[k].astype(F32)).astype(BF16)
+            far_copy(o).start()
+
+        each(1, nk, combine)
+        forward_all()
 
         lx = lax.broadcasted_iota(jnp.int32, (1, clip_lanes), 1)
         x_low, x_high = (lx >= plane).astype(F32), (lx < clip_lanes - plane).astype(F32)
@@ -530,19 +564,6 @@
             xs[q, 2 * dblk:3 * dblk] = (
                 pltpu.roll(xf, clip_lanes - plane, axis=1) * x_high).astype(BF16)
 
-
-        def g_forward(q):
-            return remote(gall.at[q, core], gall.at[q, core], f_s.at[0], f_r.at[q], dp,
-                          2 * chip + 1 - core)
-
-        def pass_on(o):
-            q = peer(o)
-            drain(gall.at[0, 0], g_r.at[q])
-            g_forward(q).start()
-
-        drain(gall.at[0, 0, pl.ds(0, nz - 1)], g_r.at[dp])
-        g_forward(dp).start()
-        each(1, ndp, pass_on)
 
         lh = lax.rem(lx, rows)
         lc = lax.rem(lx, plane)
@@ -605,25 +626,31 @@
             drain(hrow.at[others, pl.ds(0, line)], e_s.at[1])
 
         totals = []
-        for j in range(len(cuts)):
-            drain(asend[j].at[0], a_r.at[2 * j + 1])
-            acc2[j][kz, par] = acc2[j][kz, par] + arecv[j][kz].astype(F32)
-            drain(brecv[j].at[pl.ds(0, nk - 1)], b_r.at[j])
-
-            def add(o):
-                acc2[j][kz, par] = (acc2[j][kz, par]
-                                    + brecv[j][lax.rem(kz + o, nk)].astype(F32))
-
-            each(1, nk, add)
-            totals.append(acc2[j][kz, par])
+        drain(asend.at[0], a_r.at[1])
+        acc2[0][kz, par] = acc2[0][kz, par] + arecv[kz].astype(F32)
+        drain(brecv.at[pl.ds(0, nk - 1)], b_r.at[0])
+
+        def add(o):
+            acc2[0][kz, par] = (acc2[0][kz, par]
+                                     + brecv[lax.rem(kz + o, nk)].astype(F32))
+
+        each(1, nk, add)
+        totals.append(acc2[0][kz, par])
+        if len(cuts) > 1:
+            drain(rall.at[pl.ds(0, nz - 1)], r_r.at[0])
+            total = acc2[1][kz, par]
+            for o in range(1, nz):
+                total = total + rall[differ(chip, o, nz)].astype(F32)
+            totals.append(total)
         total = jnp.concatenate(totals, axis=1)
         for a in range(3):
             for bc in range(9):
                 o2[a * 9 + bc] = total[a * mblk:(a + 1) * mblk, bc * vblk:(bc + 1) * vblk]
-        for j in range(len(cuts)):
-            drain(asend[j].at[pl.ds(0, nk - 1)], a_s.at[2 * j])
-            drain(asend[j].at[0], a_s.at[2 * j + 1])
-            drain(brecv[j].at[pl.ds(0, nk - 1)], b_s.at[j])
+        if len(cuts) > 1:
+            drain(rall.at[pl.ds(0, nz - 1)], r_s.at[0])
+        drain(asend.at[pl.ds(0, nk - 1)], a_s.at[0])
+        drain(asend.at[0], a_s.at[1])
+        drain(brecv.at[pl.ds(0, nk - 1)], b_s.at[0])
 
     return kernel
 
@@ -707,13 +734,14 @@
         pltpu.VMEM((ndp, cblk, n), BF16),
         pltpu.VMEM((ndp, 2, nz, cblk, n), BF16),
         pltpu.VMEM((9 * cblk, 3 * dblk), F32),
-        [[pltpu.VMEM((nz // 2, 2, 3 * mblk, size), BF16) for _, size in cuts] for _ in range(2)]
-        + [[pltpu.VMEM((nz // 2, 3 * mblk, size), BF16) for _, size in cuts] for _ in range(4)]
-        + [[pltpu.VMEM((nz // 2, 2, 3 * mblk, size), F32) for _, size in cuts]],
+        pltpu.VMEM((nz // 2, 2, 3 * mblk, cuts[-1][1]), BF16),
+        pltpu.VMEM((nz, 3 * mblk, cuts[-1][1]), BF16),
+    ] + [pltpu.VMEM((nz // 2, 3 * mblk, cuts[0][1]), BF16)] * 4 + [
+        [[pltpu.VMEM((nz // 2, 2, 3 * mblk, size), kind) for _, size in cuts]
+         for kind in (BF16, BF16, F32, F32)],
         dma(14), dma(2), dma(2), dma(1), dma(1), dma(1), dma(1), dma(1), dma(1), dma(1), dma(ndp),
         dma(1), dma(1), dma(2), dma(2), dma(1), dma(ndp), dma(1), dma(ndp), dma(1), dma(ndp),
-        dma(len(cuts)), dma(len(cuts)), dma(2 * len(cuts)), dma(2 * len(cuts)),
-        dma(len(cuts)), dma(len(cuts)),
+        dma(len(cuts)), dma(len(cuts)), dma(1), dma(1), dma(2), dma(2), dma(1), dma(1),
     ]
     first, second = pl.pallas_call(
         make_kernel(dims),

time: 34.9 us -> 34.1 us (0.977); the launches traced: 34.3 us -> 33.9 us
  no operation moved by 1% of the time
where the time goes in v4:
time: 34.1 us; the launch traced here: 33.9 us
  Pallas kernels  33.3 us (98%)
  between operations  0.64 us (2%)
    pallas_call x1, Pallas kernels, per_device(): pl.pallas_call(make_kernel(dims), out_shape=(pltpu.VMEM((27 * cblk, dblk)...  32.4 us
    pallas_call x1, Pallas kernels, per_device(): pl.pallas_call(flush, out_shape=(jax.ShapeDtypeStruct(first.shape, F32),...  0.85 us

profile of v4, /device:TPU:0, one launch (start us, length us, event | category | flops | bytes accessed | tf_op | source)
XLA Modules:
  0.0 33.9 jit_solution(8956316666397189703)
XLA Ops:
  0.6 32.4 %step.1 = (f32[864,64]{1,0:T(8,128)S(1)}, f32[27,16,96]{2,1,0:T(8,128)S(1)}) custom-call(bf16[2,16,4,512]{3,2,1,0:T(4,128)(2,1)} %bitcast.11, bf16[13824,128]{1,0:T(8,128)(2,1)} %bitcast.8, f32[1,128]{1,0:T(1,128)} %bitcast.12, bf16[3456,384]{1,0:T(8,128)(2,1)} %bitcast.9, f32[384]{0:T(512)} %b2_hbm.1, bf16[16,2,4,1536]{3,2,1,0:T(4,128)(2,1)} %bitcast.10, ...), custom_call_target="tpu_custom_call" | custom-call | tf_op jit(solution)/shard_map/step/pallas_call | solution.py:746
  33.1 0.9 %flush.1 = (f32[864,64]{1,0:T(8,128)}, f32[27,16,96]{2,1,0:T(8,128)}) custom-call(f32[864,64]{1,0:T(8,128)S(1)} %get-tuple-element.6.a, f32[27,16,96]{2,1,0:T(8,128)S(1)} %get-tuple-element.7.b), custom_call_target="tpu_custom_call" | custom-call | tf_op jit(solution)/shard_map/flush/pallas_call | solution.py:758

commit v5 on v4

--- a/solution.py
+++ b/solution.py
@@ -49,12 +49,15 @@
                hsend, hraw, vfield, tgt, cell, psend, praw,
                hrow, lhs, csend, call_, stack, gsend, gall, acc1, rsend, rall, asend, arecv, bsend, brecv,
                chunks,
-               wsem, th_s, th_r, h_s, h_r, p_s, p_r, xz_s, xz_r, xd_s, xd_r, ht_s, ht_r, e_s, e_r,
-               c_s, c_r, g_s, g_r, f_s, f_r, q_s, q_r, r_s, r_r, a_s, a_r, b_s, b_r):
+               wsem, th_s, th_r, h_s, h_r, p_r, xz_r, xd_r, ht_r, e_r,
+               c_r, g_r, f_r, q_r, r_r, a_r, b_r):
         dp = lax.axis_index("dp")
         seq = lax.axis_index("seq")
         me = dp * nseq + seq
         chip, core = seq // 2, lax.rem(seq, 2)
+        p_s, xz_s, xd_s, ht_s, c_s, g_s, f_s, r_s, b_s = [
+            wsem.at[pl.ds(k, 1)] for k in range(9)]
+        e_s, q_s, a_s = [wsem.at[pl.ds(k, 2)] for k in (9, 11, 13)]
         qsend, qrecv, acc2, acc3 = chunks
 
         def remote(src, dst, ss, rs, d, s):
@@ -541,18 +544,7 @@
                 continue
             asend[...] = (acc2[j][:, 1 - par] + qrecv[j][:, 1 - par].astype(F32)).astype(BF16)
             each(1, nk, lambda o: near_copy(lax.rem(kz + o, nk)).start())
-            last_copy().start()
             acc2[j][:, par] = acc2[j][:, par] + qrecv[j][:, par].astype(F32)
-        drain(asend.at[pl.ds(0, nk - 1)], a_r.at[0])
-
-        def combine(o):
-            k = lax.rem(kz + o, nk)
-            bsend[k] = (acc2[0][k, par] + arecv[k].astype(F32)).astype(BF16)
-            far_copy(o).start()
-
-        each(1, nk, combine)
-        forward_all()
-
         lx = lax.broadcasted_iota(jnp.int32, (1, clip_lanes), 1)
         x_low, x_high = (lx >= plane).astype(F32), (lx < clip_lanes - plane).astype(F32)
 
@@ -564,12 +556,23 @@
             xs[q, 2 * dblk:3 * dblk] = (
                 pltpu.roll(xf, clip_lanes - plane, axis=1) * x_high).astype(BF16)
 
+        turn_clip(dp)
+        acc1[...] = jnp.zeros_like(acc1)
+        forward_all()
+        drain(asend.at[pl.ds(0, nk - 1)], a_r.at[0])
+
+        def combine(o):
+            k = lax.rem(kz + o, nk)
+            bsend[k] = (acc2[0][k, par] + arecv[k].astype(F32)).astype(BF16)
+            far_copy(o).start()
+
+        each(1, nk, combine)
+        last_copy().start()
 
         lh = lax.rem(lx, rows)
         lc = lax.rem(lx, plane)
         g_h = ((lh < rows - 1).astype(F32), None, (lh > 0).astype(F32))
         g_w = ((lc < plane - rows).astype(F32), None, (lc >= rows).astype(F32))
-        acc1[...] = jnp.zeros_like(acc1)
 
         def one_first(q):
             g = jnp.concatenate([gall[q, s % 2, s // 2].astype(F32) for s in range(nseq)], axis=1)
@@ -583,7 +586,6 @@
             acc1[...] += lax.dot_general(jnp.concatenate(grid, axis=0), xs[q], NT,
                                          preferred_element_type=F32)
 
-        turn_clip(dp)
         drain(gall.at[0, 0], f_r.at[dp])
         one_first(dp)
 
@@ -739,9 +741,8 @@
     ] + [pltpu.VMEM((nz // 2, 3 * mblk, cuts[0][1]), BF16)] * 4 + [
         [[pltpu.VMEM((nz // 2, 2, 3 * mblk, size), kind) for _, size in cuts]
          for kind in (BF16, BF16, F32, F32)],
-        dma(14), dma(2), dma(2), dma(1), dma(1), dma(1), dma(1), dma(1), dma(1), dma(1), dma(ndp),
-        dma(1), dma(1), dma(2), dma(2), dma(1), dma(ndp), dma(1), dma(ndp), dma(1), dma(ndp),
-        dma(len(cuts)), dma(len(cuts)), dma(1), dma(1), dma(2), dma(2), dma(1), dma(1),
+        dma(15), dma(2), dma(2), dma(1), dma(1), dma(1), dma(1), dma(ndp), dma(1), dma(2),
+        dma(ndp), dma(ndp), dma(ndp), dma(len(cuts)), dma(1), dma(2), dma(1),
     ]
     first, second = pl.pallas_call(
         make_kernel(dims),

time: 34.1 us -> 33.5 us (0.982)
  Pallas kernels: 33.3 us -> 32.7 us
    pallas_call x1, Pallas kernels: 32.4 us -> 31.9 us  [per_device(): pl.pallas_call(make_kernel(dims), out_shape=(pltpu.VMEM((27 * cblk, dblk)...]
where the time goes in v5:
time: 33.5 us; the launch traced here: 33.4 us
  Pallas kernels  32.7 us (98%)
  between operations  0.64 us (2%)
    pallas_call x1, Pallas kernels, per_device(): pl.pallas_call(make_kernel(dims), out_shape=(pltpu.VMEM((27 * cblk, dblk)...  31.9 us
    pallas_call x1, Pallas kernels, per_device(): pl.pallas_call(flush, out_shape=(jax.ShapeDtypeStruct(first.shape, F32),...  0.85 us

profile of v5, /device:TPU:0, one launch (start us, length us, event | category | flops | bytes accessed | tf_op | source)
XLA Modules:
  0.0 33.4 jit_solution(8164277955931875444)
XLA Ops:
  0.6 31.9 %step.1 = (f32[864,64]{1,0:T(8,128)S(1)}, f32[27,16,96]{2,1,0:T(8,128)S(1)}) custom-call(bf16[2,16,4,512]{3,2,1,0:T(4,128)(2,1)} %bitcast.11, bf16[13824,128]{1,0:T(8,128)(2,1)} %bitcast.8, f32[1,128]{1,0:T(1,128)} %bitcast.12, bf16[3456,384]{1,0:T(8,128)(2,1)} %bitcast.9, f32[384]{0:T(512)} %b2_hbm.1, bf16[16,2,4,1536]{3,2,1,0:T(4,128)(2,1)} %bitcast.10, ...), custom_call_target="tpu_custom_call" | custom-call | tf_op jit(solution)/shard_map/step/pallas_call | solution.py:747
  32.5 0.9 %flush.1 = (f32[864,64]{1,0:T(8,128)}, f32[27,16,96]{2,1,0:T(8,128)}) custom-call(f32[864,64]{1,0:T(8,128)S(1)} %get-tuple-element.6.a, f32[27,16,96]{2,1,0:T(8,128)S(1)} %get-tuple-element.7.b), custom_call_target="tpu_custom_call" | custom-call | tf_op jit(solution)/shard_map/flush/pallas_call | solution.py:759

commit v6 on v5

--- a/solution.py
+++ b/solution.py
@@ -444,18 +444,18 @@
 
         each(1, ndp - 1, lambda o: other_clip(o, pl.multiple_of(o * tile, 128)))
 
-        def half(k, j, part):
-            span = slice(part * ndp * tile, (part + 1) * ndp * tile)
+        def half(k, j, first_part, last_part):
+            depth = (last_part - first_part) * ndp * tile
+            span = slice(first_part * ndp * tile, last_part * ndp * tile)
             block = jnp.concatenate(
-                [lhs[2 * s + k, :, :, span].reshape(3 * mblk, ndp * tile) for s in range(nz)],
+                [lhs[2 * s + k, :, :, span].reshape(3 * mblk, depth) for s in range(nz)],
                 axis=0)
             low, size = cuts[j]
             return lax.dot_general(block, stack[low:low + size, span], NT,
                                    preferred_element_type=F32).reshape(nk, 2, 3 * mblk, size)
 
         for j in range(len(cuts)):
-            acc3[j][...] = half(1 - core, j, 0)
-            acc2[j][...] = half(core, j, 0)
+            acc3[j][...] = half(1 - core, j, 0, 1)
 
         drain(praw.at[pl.ds(0, nseq - 1)], p_r.at[0])
         got = praw[...].reshape(nseq * he * chunk, mid)
@@ -498,7 +498,7 @@
         swaps = [remote(qs, qr, q_s.at[j], q_r.at[j], dp, 2 * chip + 1 - core)
                  for j, (qs, qr) in enumerate(zip(qsend, qrecv))]
         for j in range(len(cuts)):
-            qsend[j][...] = (acc3[j][...] + half(1 - core, j, 1)).astype(BF16)
+            qsend[j][...] = (acc3[j][...] + half(1 - core, j, 1, 2)).astype(BF16)
             swaps[j].start()
         par, kz = lax.rem(chip, 2), chip // 2
 
@@ -535,7 +535,7 @@
                           dp, 2 * t + core)
 
         for j in range(len(cuts)):
-            acc2[j][...] = acc2[j][...] + half(core, j, 1)
+            acc2[j][...] = half(core, j, 0, 2)
             swaps[j].wait_recv()
             if j > 0:
                 rsend[...] = (acc2[j][...] + qrecv[j][...].astype(F32)).astype(BF16)

time: 33.5 us -> 33.2 us (level)
  no operation moved by 1% of the time
where the time goes in v6:
time: 33.2 us; the launch traced here: 33.1 us
  Pallas kernels  32.4 us (98%)
  between operations  0.64 us (2%)
    pallas_call x1, Pallas kernels, per_device(): pl.pallas_call(make_kernel(dims), out_shape=(pltpu.VMEM((27 * cblk, dblk)...  31.6 us
    pallas_call x1, Pallas kernels, per_device(): pl.pallas_call(flush, out_shape=(jax.ShapeDtypeStruct(first.shape, F32),...  0.85 us

profile of v6, /device:TPU:0, one launch (start us, length us, event | category | flops | bytes accessed | tf_op | source)
XLA Modules:
  0.0 33.1 jit_solution(18199156259973256298)
XLA Ops:
  0.6 31.6 %step.1 = (f32[864,64]{1,0:T(8,128)S(1)}, f32[27,16,96]{2,1,0:T(8,128)S(1)}) custom-call(bf16[2,16,4,512]{3,2,1,0:T(4,128)(2,1)} %bitcast.11, bf16[13824,128]{1,0:T(8,128)(2,1)} %bitcast.8, f32[1,128]{1,0:T(1,128)} %bitcast.12, bf16[3456,384]{1,0:T(8,128)(2,1)} %bitcast.9, f32[384]{0:T(512)} %b2_hbm.1, bf16[16,2,4,1536]{3,2,1,0:T(4,128)(2,1)} %bitcast.10, ...), custom_call_target="tpu_custom_call" | custom-call | tf_op jit(solution)/shard_map/step/pallas_call | solution.py:747
  32.2 0.9 %flush.1 = (f32[864,64]{1,0:T(8,128)}, f32[27,16,96]{2,1,0:T(8,128)}) custom-call(f32[864,64]{1,0:T(8,128)S(1)} %get-tuple-element.6.a, f32[27,16,96]{2,1,0:T(8,128)S(1)} %get-tuple-element.7.b), custom_call_target="tpu_custom_call" | custom-call | tf_op jit(solution)/shard_map/flush/pallas_call | solution.py:759

commit v7 on v6

--- a/solution.py
+++ b/solution.py
@@ -262,13 +262,6 @@
 
         drain(hraw.at[pl.ds(0, nseq - 1)], h_r.at[0])
 
-        def xz_copy(o):
-            s = lax.rem(seq + o, nseq)
-            return remote(xbuf.at[s], xall.at[dp, seq], xz_s.at[0], xz_r.at[0], dp, s)
-
-        each(1, nseq, lambda o: xz_copy(o).start())
-        xall[dp, seq] = xbuf[seq]
-
         hin = hraw[...].astype(F32)
         hext = jnp.concatenate(
             [hin[:, hh].reshape(line, mid) for hh in range(he)], axis=0)
@@ -288,6 +281,13 @@
             return remote(mine, mine, ht_s.at[0], ht_r.at[0], d, seq)
 
         each(1, ndp, lambda o: ht_copy(o).start())
+
+        def xz_copy(o):
+            s = lax.rem(seq + o, nseq)
+            return remote(xbuf.at[s], xall.at[dp, seq], xz_s.at[0], xz_r.at[0], dp, s)
+
+        each(1, nseq, lambda o: xz_copy(o).start())
+        xall[dp, seq] = xbuf[seq]
 
         cots = []
         for ij in range(4):

time: 33.2 us -> 33.4 us (level)
  no operation moved by 1% of the time
where the time goes in v7:
time: 33.4 us; the launch traced here: 33.2 us
  Pallas kernels  32.6 us (98%)
  between operations  0.64 us (2%)
    pallas_call x1, Pallas kernels, per_device(): pl.pallas_call(make_kernel(dims), out_shape=(pltpu.VMEM((27 * cblk, dblk)...  31.7 us
    pallas_call x1, Pallas kernels, per_device(): pl.pallas_call(flush, out_shape=(jax.ShapeDtypeStruct(first.shape, F32),...  0.85 us

profile of v7, /device:TPU:0, one launch (start us, length us, event | category | flops | bytes accessed | tf_op | source)
XLA Modules:
  0.0 33.2 jit_solution(10746939611668020574)
XLA Ops:
  0.6 31.7 %step.1 = (f32[864,64]{1,0:T(8,128)S(1)}, f32[27,16,96]{2,1,0:T(8,128)S(1)}) custom-call(bf16[2,16,4,512]{3,2,1,0:T(4,128)(2,1)} %bitcast.11, bf16[13824,128]{1,0:T(8,128)(2,1)} %bitcast.8, f32[1,128]{1,0:T(1,128)} %bitcast.12, bf16[3456,384]{1,0:T(8,128)(2,1)} %bitcast.9, f32[384]{0:T(512)} %b2_hbm.1, bf16[16,2,4,1536]{3,2,1,0:T(4,128)(2,1)} %bitcast.10, ...), custom_call_target="tpu_custom_call" | custom-call | tf_op jit(solution)/shard_map/step/pallas_call | solution.py:747
  32.4 0.9 %flush.1 = (f32[864,64]{1,0:T(8,128)}, f32[27,16,96]{2,1,0:T(8,128)}) custom-call(f32[864,64]{1,0:T(8,128)S(1)} %get-tuple-element.6.a, f32[27,16,96]{2,1,0:T(8,128)S(1)} %get-tuple-element.7.b), custom_call_target="tpu_custom_call" | custom-call | tf_op jit(solution)/shard_map/flush/pallas_call | solution.py:759
